TPU v7x, 256 devices: a whole 4x4x8 slice. The times are simulated.
256 devices in a mesh: chain: 64 (over y, x, z_hi, core), sector: 4 (over z_lo).
Axes of the slice: x: 4, y: 4, z: 8 (z_hi: 2, z_lo: 4; z = z_hi * 4 + z_lo), core: 2. Of those that a mesh axis runs over, the one named last changes fastest.
Arguments:
- psi: float32 [64, 16, 256, 256], P('chain', 'sector'), may hold values from -6 to 6
- kept_rank: int32 [64, 16], P('chain', 'sector'), may hold values from 64 to 256, as said below
- step_size: float32 [64, 3], P('chain'), may hold values from 0.2 to 0.6
- left_env: bfloat16 [64, 2, 16, 256, 256], P('chain', None, 'sector'), may hold values from -0.375 to 0.375
- right_env: bfloat16 [64, 2, 16, 256, 256], P('chain', None, 'sector'), may hold values from -0.375 to 0.375
- hop_left: bfloat16 [64, 2, 16, 256, 256], P('chain', None, 'sector'), may hold values from -0.375 to 0.375
- hop_right: bfloat16 [64, 2, 16, 256, 256], P('chain', None, 'sector'), may hold values from -0.375 to 0.375
- hop_source: int32 [2, 16], replicated, may hold values from 0 to 15, each once within a row
Outputs:
- site_state: float32 [64, 16, 256, 256], P('chain', 'sector')
- merged_left: float32 [64, 2, 16, 256, 256], P('chain', None, 'sector')
- merged_right: float32 [64, 2, 16, 256, 256], P('chain', None, 'sector')
Inputs may be any that keep to these rules, and one draw needn't show every extreme that they name: `kept_rank`: each partition has one sector whose kept rank is the full 256.
All inputs are finite; a program needn't handle non-finite values.
Results may differ from a plain program's by a relative error of at most 0.009.
Values may be sent and summed in bfloat16 or wider, within the bound.
A program may use at most 64 MiB of HBM per device.

v0:
```python
import jax
import jax.numpy as jnp
from jax import lax
from jax.sharding import PartitionSpec as P

STEPS = 3


def sent_to_all(array, axis):
    size = lax.axis_size(axis)
    return lax.all_to_all(
        jnp.broadcast_to(array[None], (size, *array.shape)), axis, 0, 0, tiled=True
    )


def in_order(parts, dim):
    shape = list(parts.shape[1:])
    shape[dim] *= parts.shape[0]
    return jnp.moveaxis(parts, 0, dim).reshape(shape)


def gather_directly(array, axis, dim):
    parts = sent_to_all(array, axis)
    return in_order(parts, dim)


def of_everyone(array, axis):
    return sent_to_all(array, axis).sum(axis=0)


def packed_total(arrays, axis):
    line, at, finished = (jnp.concatenate([a.reshape(-1) for a in arrays]), 0, [])
    so_far = of_everyone(line, axis)
    for a in arrays:
        finished.append(so_far[at : at + a.size].reshape(a.shape))
        at += a.size
    return tuple(finished)


def from_behind(value, axis, steps):
    count = lax.axis_size(axis)
    initial, last = (max(0, -steps), min(count, count - steps))
    return lax.ppermute(value, axis, [(source, source + steps) for source in range(initial, last)])


def on_device(psi, kept_rank, step_size, left_env, right_env, hop_left, hop_right, hop_source):
    f32 = jnp.float32
    bf16 = jnp.bfloat16
    sec_count = psi.shape[1]
    block_size = psi.shape[2]
    chi_total = sec_count * lax.axis_size("sector") * block_size
    first_sector = lax.axis_index("sector") * sec_count
    sources = lax.dynamic_slice_in_dim(hop_source, first_sector, sec_count, 1)
    row_index = lax.broadcasted_iota(jnp.int32, (sec_count, block_size), 1)
    kept_rows = (row_index < kept_rank[0][:, None]).astype(f32)
    mask = kept_rows[:, :, None] * kept_rows[:, None, :]
    left_one = left_env[0]
    right_one = right_env[0]
    hop_first = hop_left[0]
    hop_second = hop_right[0]
    state = psi[0] * mask
    for step in range(STEPS):
        state_b = state.astype(bf16)
        inner = jnp.einsum("atij,tjk->atik", left_one, state_b, preferred_element_type=f32).astype(
            bf16
        )
        image = jnp.einsum("atik,atkl->til", inner, right_one, preferred_element_type=f32)
        gathered = gather_directly(state_b, "sector", 0)
        picked = gathered[sources]
        hop_inner = jnp.einsum(
            "btij,btjk->btik", hop_first, picked, preferred_element_type=f32
        ).astype(bf16)
        image = (
            image + jnp.einsum("btik,btkl->til", hop_inner, hop_second, preferred_element_type=f32)
        ) * mask
        step_now = step_size[0, step]
        self_dot, cross, image_dot = packed_total(
            (jnp.sum(state * state), jnp.sum(state * image), jnp.sum(image * image)), "sector"
        )
        quotient = cross / self_dot
        state_resid = cross - quotient * self_dot
        resid_dot = image_dot - 2.0 * quotient * cross + quotient * quotient * self_dot
        new_dot = self_dot - 2.0 * step_now * state_resid + step_now * step_now * resid_dot
        state = state - step_now * (image - quotient * state)
        state = state / jnp.sqrt(new_dot)
    final_b = state.astype(bf16)
    left_half = jnp.einsum("tji,atjk->atik", final_b, left_one, preferred_element_type=f32).astype(
        bf16
    )
    right_half = jnp.einsum(
        "atij,tkj->atik", right_one, final_b, preferred_element_type=f32
    ).astype(bf16)
    left_own = chi_total * jnp.einsum(
        "atik,tkl->atil", left_half, final_b, preferred_element_type=f32
    )
    right_own = chi_total * jnp.einsum(
        "tij,atjk->atik", final_b, right_half, preferred_element_type=f32
    )
    left_new = from_behind(left_own.astype(jnp.bfloat16), "chain", 1).astype(left_own.dtype)
    right_new = from_behind(right_own.astype(jnp.bfloat16), "chain", -1).astype(right_own.dtype)
    merged_left = left_one.astype(f32) + left_new
    merged_right = right_one.astype(f32) + right_new
    return (state[None], merged_left[None], merged_right[None])


def solution(mesh):
    placed = (
        P("chain", "sector", None, None),
        P("chain", "sector"),
        P("chain", None),
        P("chain", None, "sector", None, None),
        P("chain", None, "sector", None, None),
        P("chain", None, "sector", None, None),
        P("chain", None, "sector", None, None),
        P(),
    )
    return jax.shard_map(
        on_device,
        mesh=mesh,
        in_specs=placed,
        out_specs=(
            P("chain", "sector", None, None),
            P("chain", None, "sector", None, None),
            P("chain", None, "sector", None, None),
        ),
        check_vma=False,
    )
```

profile of v0, /device:TPU:40, one launch (start us, length us, event | category | flops | bytes accessed | tf_op | source)
XLA Modules:
  0.0 323.8 jit_solution(11834866203374657620)
XLA Ops:
  0.6 0.0 copy-start
  0.6 0.8 fusion.55
  1.5 1.4 fusion.38
  2.9 1.5 broadcast_in_dim.23
  4.4 6.1 %all-to-all-start = ((bf16[4,4,256,256]{3,2,1,0:T(8,128)(2,1)}), bf16[4,4,256,256]{3,2,1,0:T(8,128)(2,1)}, u32[]{:S(2)}, u32[]{:S(2)}) async-start(bf16[4,4,256,256]{3,2,1,0:T(8,128)(2,1)} %broadcast_in_dim.23), calls=%async_computation | async-start | bytes 4194304 | tf_op jit(solution)/shard_map/all_to_all | solution.py:11
  10.6 0.0 copy-done.8
  10.6 0.1 compare_select_fusion
  10.6 0.1 reshape.156
  10.7 0.0 copy-done.5
  10.7 0.5 copy.138
  11.2 1.5 copy.136
  12.7 0.0 copy-done.7
  12.8 0.0 copy-start.2
  12.8 0.7 fusion.59
  14.6 40.9 %all-to-all-done = bf16[4,4,256,256]{3,2,1,0:T(8,128)(2,1)} async-done(((bf16[4,4,256,256]{3,2,1,0:T(8,128)(2,1)}), bf16[4,4,256,256]{3,2,1,0:T(8,128)(2,1)}, u32[]{:S(2)}, u32[]{:S(2)}) %all-to-all-start) | async-done | bytes 2097184 | tf_op jit(solution)/shard_map/all_to_all | solution.py:11
  55.5 3.2 gather_fusion
  58.6 0.0 copy-done
  58.7 3.3 %fusion.2 = f32[4,256,256]{2,1,0:T(8,128)} fusion(bf16[2,4,256,256]{3,2,1,0:T(8,128)(2,1)} %bitcast.214, bf16[1,2,4,256,256]{4,3,2,1,0:T(8,128)(2,1)S(1)} %copy-done, bf16[1,2,4,256,256]{4,3,2,1,0:T(8,128)(2,1)} %param.13), kind=kOutput, calls=%fused_computation.21 | convolution fusion | flops 537395200 | bytes 4194304 | tf_op jit(solution)/shard_map/btik,btkl->til/dot_general | solution.py:74
  62.0 4.7 %multiply_reduce_fusion.8 = (f32[]{:T(128)}, f32[]{:T(128)}, f32[]{:T(128)}, f32[4,256,256]{2,1,0:T(8,128)}) fusion(f32[1,4,256,256]{3,2,1,0:T(8,128)} %param.8, f32[4,256]{1,0:T(4,128)S(1)} %fusion.55, f32[4,256,256]{2,1,0:T(8,128)} %fusion.2, bf16[2,4,256,256]{2,3,0,1:T(8,128)(2,1)S(1)} %copy.138, bf16[2,4,256,256]{2,3,0,1:T(8,128)(2,1)S(1)} %copy.136), kind=kOutput, calls=%fused_computation.55 | convolution fusion | flops 540803072 | bytes 5246988 | tf_op jit(solution)/shard_map/atik,atkl->til/dot_general | solution.py:67
  66.7 2.0 pad_maximum_fusion
  68.7 0.6 broadcast_in_dim.25
  69.3 6.6 %all-to-all-start.1 = ((f32[4,1,3]{2,1,0:T(1,128)}), f32[4,1,3]{2,1,0:T(1,128)S(1)}, u32[]{:S(2)}, u32[]{:S(2)}) async-start(f32[4,1,3]{2,1,0:T(1,128)} %broadcast_in_dim.25), calls=%async_computation.1 | async-start | bytes 4096 | tf_op jit(solution)/shard_map/all_to_all | solution.py:11
  76.4 3.5 %all-to-all-done.1 = f32[4,1,3]{2,1,0:T(1,128)S(1)} async-done(((f32[4,1,3]{2,1,0:T(1,128)}), f32[4,1,3]{2,1,0:T(1,128)S(1)}, u32[]{:S(2)}, u32[]{:S(2)}) %all-to-all-start.1) | async-done | bytes 80 | tf_op jit(solution)/shard_map/all_to_all | solution.py:11
  79.9 0.6 fusion.61
  85.7 3.4 %fusion.57 = (bf16[4,256,256]{2,1,0:T(8,128)(2,1)S(1)}, f32[4,256,256]{2,1,0:T(8,128)}) fusion(f32[]{:T(128)S(6)} %sqrt.9, f32[4,256,256]{2,1,0:T(8,128)} %get-tuple-element.43, f32[]{:T(128)S(6)} %div.27, f32[]{:T(128)} %bitcast.2, f32[4,256]{1,0:T(4,128)S(1)} %fusion.55, f32[1,4,256,256]{3,2,1,0:T(8,128)} %param.8), kind=kLoop, calls=%fused_computation.82 | loop fusion | flops 2097152 | bytes 3674124 | tf_op jit(solution)/shard_map/convert_element_type | solution.py:63
  89.1 0.8 copy-done.4
  89.9 1.5 broadcast_in_dim.26
  91.4 5.8 %all-to-all-start.2 = ((bf16[4,4,256,256]{3,2,1,0:T(8,128)(2,1)}), bf16[4,4,256,256]{3,2,1,0:T(8,128)(2,1)}, u32[]{:S(2)}, u32[]{:S(2)}) async-start(bf16[4,4,256,256]{3,2,1,0:T(8,128)(2,1)} %broadcast_in_dim.26), calls=%async_computation.2 | async-start | bytes 4194304 | tf_op jit(solution)/shard_map/all_to_all | solution.py:11
  98.0 42.6 %all-to-all-done.2 = bf16[4,4,256,256]{3,2,1,0:T(8,128)(2,1)} async-done(((bf16[4,4,256,256]{3,2,1,0:T(8,128)(2,1)}), bf16[4,4,256,256]{3,2,1,0:T(8,128)(2,1)}, u32[]{:S(2)}, u32[]{:S(2)}) %all-to-all-start.2) | async-done | bytes 2097184 | tf_op jit(solution)/shard_map/all_to_all | solution.py:11
  140.6 3.2 gather_fusion.1
  143.8 3.3 %fusion.5 = f32[4,256,256]{2,1,0:T(8,128)} fusion(bf16[2,4,256,256]{3,2,1,0:T(8,128)(2,1)} %bitcast.215, bf16[1,2,4,256,256]{4,3,2,1,0:T(8,128)(2,1)S(1)} %copy-done, bf16[1,2,4,256,256]{4,3,2,1,0:T(8,128)(2,1)} %param.13), kind=kOutput, calls=%fused_computation.24 | convolution fusion | flops 537395200 | bytes 4194304 | tf_op jit(solution)/shard_map/btik,btkl->til/dot_general | solution.py:74
  147.1 4.2 %multiply_reduce_fusion.5 = (f32[]{:T(128)}, f32[]{:T(128)}, f32[]{:T(128)}, f32[4,256,256]{2,1,0:T(8,128)}) fusion(f32[4,256,256]{2,1,0:T(8,128)} %get-tuple-element.30, f32[4,256]{1,0:T(4,128)S(1)} %fusion.55, f32[4,256,256]{2,1,0:T(8,128)} %fusion.5, bf16[2,4,256,256]{2,3,0,1:T(8,128)(2,1)S(1)} %copy.138, bf16[2,4,256,256]{2,3,0,1:T(8,128)(2,1)S(1)} %copy.136, ...), kind=kOutput, calls=%fused_computation.51 | convolution fusion | flops 539754496 | bytes 5771276 | tf_op jit(solution)/shard_map/atik,atkl->til/dot_general | solution.py:67
  151.3 2.0 pad_maximum_fusion.1
  153.3 0.6 broadcast_in_dim.27
  153.9 6.6 %all-to-all-start.3 = ((f32[4,1,3]{2,1,0:T(1,128)}), f32[4,1,3]{2,1,0:T(1,128)S(1)}, u32[]{:S(2)}, u32[]{:S(2)}) async-start(f32[4,1,3]{2,1,0:T(1,128)} %broadcast_in_dim.27), calls=%async_computation.3 | async-start | bytes 4096 | tf_op jit(solution)/shard_map/all_to_all | solution.py:11
  161.8 2.7 all-to-all-done.3
  164.5 0.6 fusion.60
  169.9 3.4 %fusion.56 = (bf16[4,256,256]{2,1,0:T(8,128)(2,1)S(1)}, f32[4,256,256]{2,1,0:T(8,128)}) fusion(f32[]{:T(128)S(6)} %sqrt.10, f32[4,256,256]{2,1,0:T(8,128)} %get-tuple-element.30, f32[4,256,256]{2,1,0:T(8,128)} %get-tuple-element.44, f32[]{:T(128)S(6)} %div.30, f32[]{:T(128)} %bitcast.25), kind=kLoop, calls=%fused_computation.81 | loop fusion | flops 1572864 | bytes 3670028 | tf_op jit(solution)/shard_map/convert_element_type | solution.py:63
  173.3 0.8 copy-done.3
  174.1 1.5 broadcast_in_dim.28
  175.6 5.8 %all-to-all-start.4 = ((bf16[4,4,256,256]{3,2,1,0:T(8,128)(2,1)}), bf16[4,4,256,256]{3,2,1,0:T(8,128)(2,1)}, u32[]{:S(2)}, u32[]{:S(2)}) async-start(bf16[4,4,256,256]{3,2,1,0:T(8,128)(2,1)} %broadcast_in_dim.28), calls=%async_computation.4 | async-start | bytes 4194304 | tf_op jit(solution)/shard_map/all_to_all | solution.py:11
  182.0 42.8 %all-to-all-done.4 = bf16[4,4,256,256]{3,2,1,0:T(8,128)(2,1)} async-done(((bf16[4,4,256,256]{3,2,1,0:T(8,128)(2,1)}), bf16[4,4,256,256]{3,2,1,0:T(8,128)(2,1)}, u32[]{:S(2)}, u32[]{:S(2)}) %all-to-all-start.4) | async-done | bytes 2097184 | tf_op jit(solution)/shard_map/all_to_all | solution.py:11
  224.8 3.2 gather_fusion.2
  228.0 3.3 %fusion.8 = f32[4,256,256]{2,1,0:T(8,128)} fusion(bf16[2,4,256,256]{3,2,1,0:T(8,128)(2,1)} %bitcast.213, bf16[1,2,4,256,256]{4,3,2,1,0:T(8,128)(2,1)S(1)} %copy-done, bf16[1,2,4,256,256]{4,3,2,1,0:T(8,128)(2,1)} %param.13), kind=kOutput, calls=%fused_computation.27 | convolution fusion | flops 537395200 | bytes 4194304 | tf_op jit(solution)/shard_map/btik,btkl->til/dot_general | solution.py:74
  231.3 4.2 %multiply_reduce_fusion.2 = (f32[]{:T(128)}, f32[]{:T(128)}, f32[]{:T(128)}, f32[4,256,256]{2,1,0:T(8,128)}) fusion(f32[4,256,256]{2,1,0:T(8,128)} %get-tuple-element.28, f32[4,256]{1,0:T(4,128)S(1)} %fusion.55, f32[4,256,256]{2,1,0:T(8,128)} %fusion.8, bf16[2,4,256,256]{2,3,0,1:T(8,128)(2,1)S(1)} %copy.138, bf16[2,4,256,256]{2,3,0,1:T(8,128)(2,1)S(1)} %copy.136, ...), kind=kOutput, calls=%fused_computation.47 | convolution fusion | flops 539754496 | bytes 5771276 | tf_op jit(solution)/shard_map/atik,atkl->til/dot_general | solution.py:67
  235.5 2.0 pad_maximum_fusion.2
  237.5 0.6 broadcast_in_dim.29
  238.0 6.6 %all-to-all-start.5 = ((f32[4,1,3]{2,1,0:T(1,128)}), f32[4,1,3]{2,1,0:T(1,128)S(1)}, u32[]{:S(2)}, u32[]{:S(2)}) async-start(f32[4,1,3]{2,1,0:T(1,128)} %broadcast_in_dim.29), calls=%async_computation.5 | async-start | bytes 4096 | tf_op jit(solution)/shard_map/all_to_all | solution.py:11
  245.7 2.9 all-to-all-done.5
  248.7 0.6 fusion.58
  254.1 2.3 subtract_divide_fusion
  256.4 0.0 copy-start.1
  256.4 3.4 %fusion.9 = bf16[2,4,256,256]{2,3,0,1:T(8,128)(2,1)} fusion(bf16[2,4,256,256]{2,3,0,1:T(8,128)(2,1)} %copy-done.2, f32[4,256,256]{2,1,0:T(8,128)S(1)} %subtract_divide_fusion), kind=kOutput, calls=%fused_computation.28 | convolution fusion | flops 538968064 | bytes 3145728 | tf_op jit(solution)/shard_map/atik,tkl->atil/dot_general | solution.py:93
  259.7 1.9 collective-permute-start
  261.7 1.8 fusion.10
  263.4 10.7 %collective-permute-start.1 = (bf16[2,4,256,256]{2,3,0,1:T(8,128)(2,1)}, bf16[2,4,256,256]{2,3,0,1:T(8,128)(2,1)}, u32[]{:S(2)}, u32[]{:S(2)}) collective-permute-start(bf16[2,4,256,256]{2,3,0,1:T(8,128)(2,1)} %fusion.10), channel_id=1, source_target_pairs={{4,0},{8,4},{12,8},{16,12},{20,16},{24,20},{28,24},{32,28},{36,32}... | collective-permute-start | bytes 3145736 | tf_op jit(solution)/shard_map/ppermute | solution.py:43
  274.1 2.3 copy.100
  276.4 1.3 copy.103
  277.7 38.9 %collective-permute-done = bf16[2,4,256,256]{2,3,0,1:T(8,128)(2,1)} collective-permute-done((bf16[2,4,256,256]{2,3,0,1:T(8,128)(2,1)}, bf16[2,4,256,256]{2,3,0,1:T(8,128)(2,1)}, u32[]{:S(2)}, u32[]{:S(2)}) %collective-permute-start) | collective-permute-done | bytes 1048608 | tf_op jit(solution)/shard_map/ppermute | solution.py:43
  316.6 1.8 add_bitcast_fusion.1
  318.4 1.8 copy.133
  320.2 0.0 collective-permute-done.1
  320.2 1.8 add_bitcast_fusion
  322.0 1.8 copy.134
  (13 shorter events, 0.1 us)
Async XLA Ops:
  0.6 58.0 %copy-start = (bf16[1,2,4,256,256]{4,3,2,1,0:T(8,128)(2,1)S(1)}, bf16[1,2,4,256,256]{4,3,2,1,0:T(8,128)(2,1)}, u32[]{:S(2)}) copy-start(bf16[1,2,4,256,256]{4,3,2,1,0:T(8,128)(2,1)} %param.14) | copy-start | bytes 3145732
  4.4 6.1 %copy-start.8 = (s32[2,16]{1,0:T(2,128)S(1)}, s32[2,16]{1,0:T(2,128)}, u32[]{:S(2)}) copy-start(s32[2,16]{1,0:T(2,128)} %param.15) | copy-start | bytes 388
  4.4 6.3 %copy-start.5 = (bf16[1,2,4,256,256]{4,3,2,1,0:T(8,128)(2,1)S(1)}, bf16[1,2,4,256,256]{4,3,2,1,0:T(8,128)(2,1)}, u32[]{:S(2)}) copy-start(bf16[1,2,4,256,256]{4,3,2,1,0:T(8,128)(2,1)} %param.12) | copy-start | bytes 3145732
  4.4 51.1 %all-to-all-start = ((bf16[4,4,256,256]{3,2,1,0:T(8,128)(2,1)}), bf16[4,4,256,256]{3,2,1,0:T(8,128)(2,1)}, u32[]{:S(2)}, u32[]{:S(2)}) async-start(bf16[4,4,256,256]{3,2,1,0:T(8,128)(2,1)} %broadcast_in_dim.23), calls=%async_computation | async-start | bytes 4194304 | tf_op jit(solution)/shard_map/all_to_all | solution.py:11
  10.7 2.0 copy-start.7
  12.8 218.5 %copy-start.2 = (bf16[2,4,256,256]{2,3,0,1:T(8,128)(2,1)}, bf16[2,4,256,256]{2,3,0,1:T(8,128)(2,1)S(1)}, u32[]{:S(2)}) copy-start(bf16[2,4,256,256]{2,3,0,1:T(8,128)(2,1)S(1)} %copy.136) | copy-start | bytes 3145732
  69.3 10.6 %all-to-all-start.1 = ((f32[4,1,3]{2,1,0:T(1,128)}), f32[4,1,3]{2,1,0:T(1,128)S(1)}, u32[]{:S(2)}, u32[]{:S(2)}) async-start(f32[4,1,3]{2,1,0:T(1,128)} %broadcast_in_dim.25), calls=%async_computation.1 | async-start | bytes 4096 | tf_op jit(solution)/shard_map/all_to_all | solution.py:11
  89.1 0.8 copy-start.4
  91.4 49.2 %all-to-all-start.2 = ((bf16[4,4,256,256]{3,2,1,0:T(8,128)(2,1)}), bf16[4,4,256,256]{3,2,1,0:T(8,128)(2,1)}, u32[]{:S(2)}, u32[]{:S(2)}) async-start(bf16[4,4,256,256]{3,2,1,0:T(8,128)(2,1)} %broadcast_in_dim.26), calls=%async_computation.2 | async-start | bytes 4194304 | tf_op jit(solution)/shard_map/all_to_all | solution.py:11
  153.9 10.6 %all-to-all-start.3 = ((f32[4,1,3]{2,1,0:T(1,128)}), f32[4,1,3]{2,1,0:T(1,128)S(1)}, u32[]{:S(2)}, u32[]{:S(2)}) async-start(f32[4,1,3]{2,1,0:T(1,128)} %broadcast_in_dim.27), calls=%async_computation.3 | async-start | bytes 4096 | tf_op jit(solution)/shard_map/all_to_all | solution.py:11
  173.3 0.8 copy-start.3
  175.6 49.2 %all-to-all-start.4 = ((bf16[4,4,256,256]{3,2,1,0:T(8,128)(2,1)}), bf16[4,4,256,256]{3,2,1,0:T(8,128)(2,1)}, u32[]{:S(2)}, u32[]{:S(2)}) async-start(bf16[4,4,256,256]{3,2,1,0:T(8,128)(2,1)} %broadcast_in_dim.28), calls=%async_computation.4 | async-start | bytes 4194304 | tf_op jit(solution)/shard_map/all_to_all | solution.py:11
  238.0 10.6 %all-to-all-start.5 = ((f32[4,1,3]{2,1,0:T(1,128)}), f32[4,1,3]{2,1,0:T(1,128)S(1)}, u32[]{:S(2)}, u32[]{:S(2)}) async-start(f32[4,1,3]{2,1,0:T(1,128)} %broadcast_in_dim.29), calls=%async_computation.5 | async-start | bytes 4096 | tf_op jit(solution)/shard_map/all_to_all | solution.py:11
  256.4 5.3 %copy-start.1 = (f32[4,256,256]{2,1,0:T(8,128)}, f32[4,256,256]{2,1,0:T(8,128)S(1)}, u32[]{:S(2)}) copy-start(f32[4,256,256]{2,1,0:T(8,128)S(1)} %subtract_divide_fusion) | copy-start | bytes 3145732
  259.7 56.9 %collective-permute-start = (bf16[2,4,256,256]{2,3,0,1:T(8,128)(2,1)}, bf16[2,4,256,256]{2,3,0,1:T(8,128)(2,1)}, u32[]{:S(2)}, u32[]{:S(2)}) collective-permute-start(bf16[2,4,256,256]{2,3,0,1:T(8,128)(2,1)} %fusion.9), channel_id=1, source_target_pairs={{0,4},{4,8},{8,12},{12,16},{16,20},{20,24},{24,28},{28,32},{32,36}... | collective-permute-start | bytes 3145736 | tf_op jit(solution)/shard_map/ppermute | solution.py:43
  263.4 13.0 %copy-start.6 = (bf16[1,2,4,256,256]{4,3,2,1,0:T(8,128)(2,1)S(1)}, bf16[1,2,4,256,256]{4,3,2,1,0:T(8,128)(2,1)}, u32[]{:S(2)}) copy-start(bf16[1,2,4,256,256]{4,3,2,1,0:T(8,128)(2,1)} %param.12) | copy-start | bytes 3145732
  263.4 56.8 %collective-permute-start.1 = (bf16[2,4,256,256]{2,3,0,1:T(8,128)(2,1)}, bf16[2,4,256,256]{2,3,0,1:T(8,128)(2,1)}, u32[]{:S(2)}, u32[]{:S(2)}) collective-permute-start(bf16[2,4,256,256]{2,3,0,1:T(8,128)(2,1)} %fusion.10), channel_id=1, source_target_pairs={{4,0},{8,4},{12,8},{16,12},{20,16},{24,20},{28,24},{32,28},{36,32}... | collective-permute-start | bytes 3145736 | tf_op jit(solution)/shard_map/ppermute | solution.py:43
where the time goes:
time: 325 us; the launch traced here: 324 us
  waiting for transfers between devices  174 us (54%)
  starting transfers between devices  50.1 us (15%)
  local copies, waits for them, and re-layouts  29.3 us (9%)
  matrix products  28.2 us (9%)
  other arithmetic  20.9 us (6%)
  between operations  20.9 us (6%)
    all_to_all x6, waiting for transfers between devices, sent_to_all(): lax.all_to_all(jnp.broadcast_to(array[None], (size, *array.shape)), axis,...  135 us
    ppermute x2, waiting for transfers between devices, from_behind(): lax.ppermute(value, axis, [(source, source + steps) for source in range(i...  38.9 us
    all_to_all x6, starting transfers between devices, sent_to_all(): lax.all_to_all(jnp.broadcast_to(array[None], (size, *array.shape)), axis,...  37.5 us
    dot_general x3, matrix products, on_device(): jnp.einsum('atik,atkl->til', inner, right_one, preferred_element_type=f32)  13.1 us
    ppermute x2, starting transfers between devices, from_behind(): lax.ppermute(value, axis, [(source, source + steps) for source in range(i...  12.6 us
    dot_general x3, matrix products, on_device(): jnp.einsum('btik,btkl->til', hop_inner, hop_second, preferred_element_typ...  9.95 us
    gather x3, local copies, waits for them, and re-layouts, on_device(): picked = gathered[sources]  9.51 us
    unnamed x22, local copies, waits for them, and re-layouts  8.83 us
  transfers between devices with their start and end apart: 8, of which 7 were waited for; matrix products, arithmetic and copies ran while one was open for 4% of the time, Pallas kernels for 0%

commit v1 on v0

v1 whole, which is shorter than its diff:
```python
import jax
import jax.numpy as jnp
from jax import lax
from jax.experimental import pallas as pl
from jax.experimental.pallas import tpu as pltpu
from jax.sharding import PartitionSpec as P

MESH = pl.DeviceIdType.MESH
STEPS = 3
OWN = 4
SLOTS = 8
CHUNKS = 4
ENTRIES = tuple((i, j) for j in range(STEPS + 1) for i in range(j + 1))


def entry(i, j):
    return ENTRIES.index((min(i, j), max(i, j)))


def pair_dot(a, b):
    rows, cols = a.shape
    return jnp.sum((a * b).reshape(rows // 8, 8, cols), axis=0)


def quadratic(coef, other, gram, row_shift, col_shift):
    total = None
    for i, a in enumerate(coef):
        for j, b in enumerate(other):
            term = a * b * gram[entry(i + row_shift, j + col_shift)]
            total = term if total is None else total + term
    return total


def kernel(
    rank, step_size, source,
    psi_hbm, left_hbm, right_hbm, hop_left_hbm, hop_right_hbm,
    state_out, from_left, from_right,
    *scratch,
):
    f32, bf16 = jnp.float32, jnp.bfloat16
    chunk_bufs = [scratch[k * CHUNKS : (k + 1) * CHUNKS] for k in range(STEPS)]
    at = STEPS * CHUNKS
    packed = scratch[at : at + STEPS]
    at += STEPS
    vec = scratch[at : at + STEPS + 1]
    at += STEPS + 1
    (psi, left, right, hop_left, hop_right, final, send_left, send_right, gram_acc, gram_in, gram_out,
     load_sem, send_sem, recv_sem, gram_send, gram_recv, merge_send, merge_recv, out_sem) = scratch[at:]

    me_c = lax.axis_index("chain")
    n_c = lax.axis_size("chain")
    z = lax.axis_index("sector")
    near = z + 1 - 2 * lax.rem(z, 2)
    peer = 3 - z
    far = 3 - near
    inner_far = jnp.where(z == 0, 2, 1)
    is_inner = jnp.logical_or(z == 1, z == 2)
    is_outer = jnp.logical_not(is_inner)
    nxt = lax.rem(me_c + 1, n_c)
    prv = lax.rem(me_c + n_c - 1, n_c)
    blk = psi.shape[1]
    rows = blk // CHUNKS
    chi = float(16 * blk)

    loads = [
        pltpu.make_async_copy(psi_hbm.at[0], psi, load_sem.at[0]),
        pltpu.make_async_copy(left_hbm.at[0], left, load_sem.at[1]),
        pltpu.make_async_copy(right_hbm.at[0], right, load_sem.at[2]),
        pltpu.make_async_copy(hop_left_hbm.at[0], hop_left, load_sem.at[3]),
        pltpu.make_async_copy(hop_right_hbm.at[0], hop_right, load_sem.at[4]),
    ]
    for copy in loads:
        copy.start()

    barrier = pltpu.get_barrier_semaphore()
    for d in range(1, 4):
        pl.semaphore_signal(barrier, inc=1, device_id=(me_c, lax.rem(z + d, 4)), device_id_type=MESH)
    for c in (prv, nxt):
        pl.semaphore_signal(barrier, inc=1, device_id=(c, z), device_id_type=MESH)

    row_at = lax.broadcasted_iota(jnp.int32, (blk, blk), 0)
    col_at = lax.broadcasted_iota(jnp.int32, (blk, blk), 1)

    def kept(j, value):
        r = rank[0, j]
        return jnp.where((row_at < r) & (col_at < r), value, 0.0)

    def put_own(k, j, value):
        value = value.astype(bf16)
        for c in range(CHUNKS):
            chunk_bufs[k][c][12 + j] = value[c * rows : (c + 1) * rows]

    def block(k, i):
        return jnp.concatenate([chunk_bufs[k][c][i] for c in range(CHUNKS)], axis=0)

    def remote(src, dst, k, c, kind, to):
        return pltpu.make_async_remote_copy(
            src_ref=src, dst_ref=dst, send_sem=send_sem.at[k, c, kind], recv_sem=recv_sem.at[k, c, kind],
            device_id=(me_c, to), device_id_type=MESH,
        )

    def to_peer(k, c):
        buf = chunk_bufs[k][c]
        return remote(buf.at[12:16], buf.at[0:4], k, c, 0, peer)

    def to_far(k, c):
        buf = chunk_bufs[k][c]
        return remote(buf.at[12:16], buf.at[4:8], k, c, 1, inner_far)

    def to_near(k, c):
        buf = chunk_bufs[k][c]
        return remote(buf.at[12:16], buf.at[8:12], k, c, 2, near)

    def to_outer(k, c):
        return remote(packed[k].at[c], chunk_bufs[k][c].at[0:SLOTS], k, c, 3, near)

    def send_own(k):
        @pl.when(is_outer)
        def _():
            for c in range(CHUNKS):
                to_far(k, c).start()
                to_near(k, c).start()

        @pl.when(is_inner)
        def _():
            for c in range(CHUNKS):
                to_peer(k, c).start()

    def owner_of(s):
        owner = s // OWN
        return owner, s - owner * OWN

    def exchange(k):
        @pl.when(is_inner)
        def _():
            picks = []
            for b in range(2):
                for j in range(OWN):
                    owner, loc = owner_of(source[b, near * OWN + j])
                    picks.append(
                        jnp.where(owner == peer, loc, jnp.where(owner == far, 4 + loc, 12 + loc))
                    )
            for c in range(CHUNKS):
                to_peer(k, c).wait_recv()
                to_far(k, c).wait_recv()
                to_near(k, c).wait_recv()
                for s, pick in enumerate(picks):
                    packed[k][c, s] = chunk_bufs[k][c][pick]
                to_outer(k, c).start()

        @pl.when(is_outer)
        def _():
            for c in range(CHUNKS):
                to_outer(k, c).wait_recv()

    def picked(b, j):
        owner, loc = owner_of(source[b, z * OWN + j])
        at_inner = jnp.where(
            owner == peer, loc, jnp.where(owner == far, 4 + loc, jnp.where(owner == near, 8 + loc, 12 + loc))
        )
        at_outer = jnp.where(owner == z, 12 + loc, b * OWN + j)
        return jnp.where(is_inner, at_inner, at_outer)

    def dot(a, b):
        return jnp.dot(a, b, preferred_element_type=f32)

    gram_acc[...] = jnp.zeros_like(gram_acc)
    loads[0].wait()

    def first(j, carry):
        value = kept(j, psi[j])
        vec[0][j] = value
        put_own(0, j, value)
        gram_acc[entry(0, 0)] += pair_dot(value, value)
        return carry

    lax.fori_loop(0, OWN, first, 0)
    pl.semaphore_wait(barrier, 5)
    send_own(0)
    for copy in loads[1:]:
        copy.wait()

    for k in range(STEPS):

        def on_site(j, carry):
            own = block(k, 12 + j)
            total = None
            for a in range(2):
                half = dot(left[a, j], own).astype(bf16)
                term = dot(half, right[a, j])
                total = term if total is None else total + term
            vec[k + 1][j] = total
            return carry

        lax.fori_loop(0, OWN, on_site, 0)
        exchange(k)

        def hop(j, carry):
            total = vec[k + 1][j]
            for b in range(2):
                half = dot(hop_left[b, j], block(k, picked(b, j))).astype(bf16)
                total = total + dot(half, hop_right[b, j])
            total = kept(j, total)
            vec[k + 1][j] = total
            if k + 1 < STEPS:
                put_own(k + 1, j, total)
            for i in range(k + 2):
                other = total if i == k + 1 else vec[i][j]
                gram_acc[entry(i, k + 1)] += pair_dot(total, other)
            return carry

        lax.fori_loop(0, OWN, hop, 0)
        if k + 1 < STEPS:
            send_own(k + 1)

    for e in range(len(ENTRIES)):
        line = jnp.sum(gram_acc[e], axis=0, keepdims=True)
        gram_out[e : e + 1, :] = line[:, :128] + line[:, 128:]
    gram_out[len(ENTRIES) :, :] = jnp.zeros((16 - len(ENTRIES), 128), f32)

    def gram_copy(d):
        return pltpu.make_async_remote_copy(
            src_ref=gram_out, dst_ref=gram_in.at[d - 1], send_sem=gram_send.at[d - 1],
            recv_sem=gram_recv.at[d - 1], device_id=(me_c, lax.rem(z + d, 4)), device_id_type=MESH,
        )

    for d in range(1, 4):
        gram_copy(d).start()
    for d in range(1, 4):
        gram_copy(d).wait_recv()
    gram_all = jnp.sum(gram_out[...] + gram_in[0] + gram_in[1] + gram_in[2], axis=1, keepdims=True)
    gram = [gram_all[e : e + 1] for e in range(len(ENTRIES))]

    coef = [jnp.ones((1, 1), f32)]
    for k in range(STEPS):
        h = step_size[0, k]
        self_dot = quadratic(coef, coef, gram, 0, 0)
        cross = quadratic(coef, coef, gram, 0, 1)
        grow = 1.0 + h * (cross / self_dot)
        new = [grow * c for c in coef] + [jnp.zeros((1, 1), f32)]
        for i, c in enumerate(coef):
            new[i + 1] = new[i + 1] - h * c
        scale = 1.0 / jnp.sqrt(quadratic(new, new, gram, 0, 0))
        coef = [c * scale for c in new]

    def merge(direction, a, j):
        src, dst, to = ((send_left, from_left, nxt), (send_right, from_right, prv))[direction]
        return pltpu.make_async_remote_copy(
            src_ref=src.at[a, j], dst_ref=dst.at[a, j], send_sem=merge_send.at[direction, a, j],
            recv_sem=merge_recv.at[direction, a, j], device_id=(to, z), device_id_type=MESH,
        )

    has_next = me_c < n_c - 1
    has_prev = me_c > 0

    def finish(j, carry):
        value = coef[0] * vec[0][j]
        for i in range(1, STEPS + 1):
            value = value + coef[i] * vec[i][j]
        final[j] = value
        own = value.astype(bf16)
        own_t = value.T.astype(bf16)
        for a in range(2):
            half = dot(own_t, left[a, j]).astype(bf16)
            send_left[a, j] = (chi * dot(half, own)).astype(bf16)
            half = dot(right[a, j], own_t).astype(bf16)
            send_right[a, j] = (chi * dot(own, half)).astype(bf16)

        @pl.when(has_next)
        def _():
            for a in range(2):
                merge(0, a, j).start()

        @pl.when(has_prev)
        def _():
            for a in range(2):
                merge(1, a, j).start()

        return carry

    lax.fori_loop(0, OWN, finish, 0)
    put_state = pltpu.make_async_copy(final, state_out.at[0], out_sem)
    put_state.start()

    for k in range(STEPS):

        @pl.when(is_outer)
        def _():
            for c in range(CHUNKS):
                to_far(k, c).wait_send()
                to_near(k, c).wait_send()

        @pl.when(is_inner)
        def _():
            for c in range(CHUNKS):
                to_peer(k, c).wait_send()
                to_outer(k, c).wait_send()

    for d in range(1, 4):
        gram_copy(d).wait_send()

    @pl.when(has_next)
    def _():
        for a in range(2):
            for j in range(OWN):
                merge(0, a, j).wait_send()
                merge(1, a, j).wait_recv()

    @pl.when(has_prev)
    def _():
        for a in range(2):
            for j in range(OWN):
                merge(1, a, j).wait_send()
                merge(0, a, j).wait_recv()

    put_state.wait()


def on_device(psi, kept_rank, step_size, left_env, right_env, hop_left, hop_right, hop_source):
    f32, bf16 = jnp.float32, jnp.bfloat16
    own, blk = psi.shape[1], psi.shape[2]
    rows = blk // CHUNKS
    env = (2, own, blk, blk)
    smem = pl.BlockSpec(memory_space=pltpu.SMEM)
    hbm = pl.BlockSpec(memory_space=pl.ANY)
    dma = pltpu.SemaphoreType.DMA
    state, from_left, from_right = pl.pallas_call(
        kernel,
        out_shape=(
            jax.ShapeDtypeStruct(psi.shape, f32),
            jax.ShapeDtypeStruct(env, bf16),
            jax.ShapeDtypeStruct(env, bf16),
        ),
        in_specs=[smem] * 3 + [hbm] * 5,
        out_specs=(hbm, hbm, hbm),
        scratch_shapes=[
            *[pltpu.VMEM((16, rows, blk), bf16) for _ in range(STEPS * CHUNKS)],
            *[pltpu.VMEM((CHUNKS, SLOTS, rows, blk), bf16) for _ in range(STEPS)],
            *[pltpu.VMEM((own, blk, blk), f32) for _ in range(STEPS + 1)],
            pltpu.VMEM((own, blk, blk), f32),
            *[pltpu.VMEM(env, bf16) for _ in range(4)],
            pltpu.VMEM((own, blk, blk), f32),
            pltpu.VMEM(env, bf16),
            pltpu.VMEM(env, bf16),
            pltpu.VMEM((len(ENTRIES), 8, blk), f32),
            pltpu.VMEM((3, 16, 128), f32),
            pltpu.VMEM((16, 128), f32),
            dma((5,)),
            dma((STEPS, CHUNKS, 4)),
            dma((STEPS, CHUNKS, 4)),
            dma((3,)),
            dma((3,)),
            dma((2, 2, own)),
            dma((2, 2, own)),
            dma,
        ],
        compiler_params=pltpu.CompilerParams(
            collective_id=0, has_side_effects=True, vmem_limit_bytes=48 * 1024 * 1024
        ),
    )(kept_rank, step_size, hop_source, psi, left_env, right_env, hop_left, hop_right)
    me_c = lax.axis_index("chain")
    last = lax.axis_size("chain") - 1
    merged_left = left_env[0].astype(f32) + jnp.where(me_c == 0, 0.0, from_left.astype(f32))
    merged_right = right_env[0].astype(f32) + jnp.where(me_c == last, 0.0, from_right.astype(f32))
    return state, merged_left[None], merged_right[None]


def solution(mesh):
    part = P("chain", "sector", None, None)
    term = P("chain", None, "sector", None, None)
    return jax.shard_map(
        on_device,
        mesh=mesh,
        in_specs=(part, P("chain", "sector"), P("chain", None), term, term, term, term, P()),
        out_specs=(part, term, term),
        check_vma=False,
    )
```

time: 325 us -> 167 us (0.51)
  waiting for transfers between devices: 174 us -> 0 us
  Pallas kernels: 0 us -> 157 us
  starting transfers between devices: 50.1 us -> 0 us
  matrix products: 28.2 us -> 0 us
  local copies, waits for them, and re-layouts: 29.3 us -> 5.4 us
  between operations: 20.9 us -> 0.67 us
  other arithmetic: 20.9 us -> 2.67 us
    pallas_call x0 -> x1, Pallas kernels: none -> 157 us  [on_device(): pl.pallas_call(kernel, out_shape=(jax.ShapeDtypeStruct(psi.shape, f32), j...]
    all_to_all x6 -> x0, waiting for transfers between devices: 135 us -> none  [sent_to_all(): lax.all_to_all(jnp.broadcast_to(array[None], (size, *array.shape)), axis,...]
    ppermute x2 -> x0, waiting for transfers between devices: 38.9 us -> none  [from_behind(): lax.ppermute(value, axis, [(source, source + steps) for source in range(i...]
    all_to_all x6 -> x0, starting transfers between devices: 37.5 us -> none  [sent_to_all(): lax.all_to_all(jnp.broadcast_to(array[None], (size, *array.shape)), axis,...]
    dot_general x8 -> x0, matrix products: 28.2 us -> none  [the longest x3 13.1 us: on_device(): jnp.einsum('atik,atkl->til', inner, right_one, preferred_element_type=f32)]
    ppermute x2 -> x0, starting transfers between devices: 12.6 us -> none  [from_behind(): lax.ppermute(value, axis, [(source, source + steps) for source in range(i...]
    gather x3 -> x0, local copies, waits for them, and re-layouts: 9.51 us -> none  [on_device(): picked = gathered[sources]]
    convert_element_type x3 -> x0, other arithmetic: 7.62 us -> none  [the longest x2 6.8 us: on_device(): state_b = state.astype(bf16)]
  transfers between devices with their start and end apart: 8 -> 0, of which waited for: 7 -> 0; matrix products, arithmetic and copies ran while one was open for 4% -> 0% of each run, Pallas kernels for 0% -> 0%
where the time goes in v1:
time: 167 us; the launch traced here: 166 us
  Pallas kernels  157 us (94%)
  local copies, waits for them, and re-layouts  5.4 us (3%)
  other arithmetic  2.67 us (2%)
    pallas_call x1, Pallas kernels, on_device(): pl.pallas_call(kernel, out_shape=(jax.ShapeDtypeStruct(psi.shape, f32), j...  157 us
    unnamed x13, local copies, waits for them, and re-layouts  5.4 us

profile of v1, /device:TPU:40, one launch (start us, length us, event | category | flops | bytes accessed | tf_op | source)
XLA Modules:
  0.0 165.8 jit_solution(13062242715445200956)
XLA Ops:
  0.6 0.0 copy-start
  0.7 1.2 copy-done
  1.9 0.0 copy-start.1
  1.9 1.2 copy-done.1
  3.1 0.0 copy-start.2
  3.1 0.7 copy-done.2
  3.8 0.0 copy-start.3
  3.8 0.7 copy-done.3
  4.4 0.0 copy-start.4
  4.4 0.7 copy-done.4
  5.1 0.0 copy-start.5
  5.1 157.0 %shard_map.103 = (f32[1,4,256,256]{3,2,1,0:T(8,128)S(1)}, bf16[2,4,256,256]{3,2,1,0:T(8,128)(2,1)S(1)}, bf16[2,4,256,256]{3,2,1,0:T(8,128)(2,1)S(1)}) custom-call(s32[1,4]{1,0:T(1,128)S(1)} %copy-done.3, f32[1,3]{1,0:T(1,128)S(1)} %copy-done.4, s32[2,16]{1,0:T(2,128)S(1)} %copy-done.2, f32[1,4,256,256]{3,2,1,0:T(8,128)S(1)} %copy-done.1, ...), custom_call_target="tpu_custom_call" | custom-call | tf_op jit(solution)/shard_map/pallas_call | solution.py:327
  162.1 0.0 copy-done.5
  162.1 2.7 %fusion = (f32[1,2,4,256,256]{4,3,2,1,0:T(8,128)}, f32[1,2,4,256,256]{4,3,2,1,0:T(8,128)}) fusion(bf16[2,4,256,256]{3,2,1,0:T(8,128)(2,1)S(1)} %get-tuple-element.8, bf16[1,2,4,256,256]{4,3,2,1,0:T(8,128)(2,1)S(1)} %copy-done.5, pred[]{:T(512)S(6)} %eq.7, bf16[2,4,256,256]{3,2,1,0:T(8,128)(2,1)S(1)} %get-tuple-element.7, pred[]{:T(512)S(6)} %eq.6, ...), kind=kLoop, calls=%fused_computation.1 | loop fusion | flops 4194304 | bytes 8388610 | tf_op jit(solution)/shard_map/broadcast_in_dim | solution.py:365
  164.8 1.0 copy.12
Async XLA Ops:
  0.6 1.2 copy-start
  1.9 1.2 copy-start.1
  3.1 0.7 copy-start.2
  3.8 0.7 copy-start.3
  4.4 0.7 copy-start.4
  5.1 157.0 %copy-start.5 = (bf16[1,2,4,256,256]{4,3,2,1,0:T(8,128)(2,1)S(1)}, bf16[1,2,4,256,256]{4,3,2,1,0:T(8,128)(2,1)}, u32[]{:S(2)}) copy-start(bf16[1,2,4,256,256]{4,3,2,1,0:T(8,128)(2,1)} %right_hbm.1) | copy-start | bytes 3145732

commit v2 on v1

--- a/solution.py
+++ b/solution.py
@@ -8,8 +8,11 @@
 MESH = pl.DeviceIdType.MESH
 STEPS = 3
 OWN = 4
-SLOTS = 8
-CHUNKS = 4
+HOPS = 2
+EARLY = 4
+CHUNKS = 8
+RELAY_LAG = CHUNKS - 2
+LATE_LAG = 2
 ENTRIES = tuple((i, j) for j in range(STEPS + 1) for i in range(j + 1))
 
 
@@ -38,13 +41,16 @@
     *scratch,
 ):
     f32, bf16 = jnp.float32, jnp.bfloat16
-    chunk_bufs = [scratch[k * CHUNKS : (k + 1) * CHUNKS] for k in range(STEPS)]
-    at = STEPS * CHUNKS
-    packed = scratch[at : at + STEPS]
-    at += STEPS
+    per = STEPS * CHUNKS
+    near_bufs = [scratch[k * CHUNKS : (k + 1) * CHUNKS] for k in range(STEPS)]
+    far_bufs = [scratch[per + k * CHUNKS : per + (k + 1) * CHUNKS] for k in range(STEPS)]
+    at = 2 * per
+    early_bufs = scratch[at : at + STEPS]
+    late_bufs = scratch[at + STEPS : at + 2 * STEPS]
+    at += 2 * STEPS
     vec = scratch[at : at + STEPS + 1]
     at += STEPS + 1
-    (psi, left, right, hop_left, hop_right, final, send_left, send_right, gram_acc, gram_in, gram_out,
+    (psi, left, right, hop_left, hop_right, final, send_left, send_right, gram_acc, gram_in, gram_out, picks,
      load_sem, send_sem, recv_sem, gram_send, gram_recv, merge_send, merge_recv, out_sem) = scratch[at:]
 
     me_c = lax.axis_index("chain")
@@ -53,7 +59,6 @@
     near = z + 1 - 2 * lax.rem(z, 2)
     peer = 3 - z
     far = 3 - near
-    inner_far = jnp.where(z == 0, 2, 1)
     is_inner = jnp.logical_or(z == 1, z == 2)
     is_outer = jnp.logical_not(is_inner)
     nxt = lax.rem(me_c + 1, n_c)
@@ -88,37 +93,41 @@
     def put_own(k, j, value):
         value = value.astype(bf16)
         for c in range(CHUNKS):
-            chunk_bufs[k][c][12 + j] = value[c * rows : (c + 1) * rows]
-
-    def block(k, i):
-        return jnp.concatenate([chunk_bufs[k][c][i] for c in range(CHUNKS)], axis=0)
-
-    def remote(src, dst, k, c, kind, to):
+            near_bufs[k][c][4 + j] = value[c * rows : (c + 1) * rows]
+
+    def own_block(k, j):
+        return jnp.concatenate([near_bufs[k][c][4 + j] for c in range(CHUNKS)], axis=0)
+
+    def chunk_of(k, c, i):
+        return jnp.where(
+            i < 8, near_bufs[k][c][jnp.minimum(i, 7)], far_bufs[k][c][jnp.maximum(i - 8, 0)]
+        )
+
+    def remote(src, dst, k, c, sent, received, to):
         return pltpu.make_async_remote_copy(
-            src_ref=src, dst_ref=dst, send_sem=send_sem.at[k, c, kind], recv_sem=recv_sem.at[k, c, kind],
+            src_ref=src, dst_ref=dst, send_sem=send_sem.at[k, c, sent], recv_sem=recv_sem.at[k, c, received],
             device_id=(me_c, to), device_id_type=MESH,
         )
 
     def to_peer(k, c):
-        buf = chunk_bufs[k][c]
-        return remote(buf.at[12:16], buf.at[0:4], k, c, 0, peer)
-
-    def to_far(k, c):
-        buf = chunk_bufs[k][c]
-        return remote(buf.at[12:16], buf.at[4:8], k, c, 1, inner_far)
+        return remote(near_bufs[k][c].at[4:8], near_bufs[k][c].at[0:4], k, c, 0, 0, peer)
 
     def to_near(k, c):
-        buf = chunk_bufs[k][c]
-        return remote(buf.at[12:16], buf.at[8:12], k, c, 2, near)
-
-    def to_outer(k, c):
-        return remote(packed[k].at[c], chunk_bufs[k][c].at[0:SLOTS], k, c, 3, near)
+        return remote(near_bufs[k][c].at[4:8], far_bufs[k][c].at[4:8], k, c, 0, 2, near)
+
+    def relay(k, c):
+        return remote(far_bufs[k][c].at[4:8], far_bufs[k][c].at[0:4], k, c, 1, 1, peer)
+
+    def early(k, c):
+        return remote(early_bufs[k].at[c], near_bufs[k][c].at[0:4], k, c, 2, 0, near)
+
+    def late(k, c):
+        return remote(late_bufs[k].at[c], far_bufs[k][c].at[0:4], k, c, 3, 1, near)
 
     def send_own(k):
         @pl.when(is_outer)
         def _():
             for c in range(CHUNKS):
-                to_far(k, c).start()
                 to_near(k, c).start()
 
         @pl.when(is_inner)
@@ -130,36 +139,77 @@
         owner = s // OWN
         return owner, s - owner * OWN
 
-    def exchange(k):
-        @pl.when(is_inner)
-        def _():
-            picks = []
-            for b in range(2):
-                for j in range(OWN):
-                    owner, loc = owner_of(source[b, near * OWN + j])
-                    picks.append(
-                        jnp.where(owner == peer, loc, jnp.where(owner == far, 4 + loc, 12 + loc))
-                    )
+    outer = jnp.where(is_inner, near, z)
+    zero, one = jnp.int32(0), jnp.int32(1)
+    middle_seen = zero
+    needed = [zero] * OWN
+    entries = []
+    for n in range(HOPS * OWN):
+        owner, loc = owner_of(source[n // OWN, outer * OWN + n % OWN])
+        is_far = owner == 3 - outer
+        is_middle = jnp.logical_not(jnp.logical_or(is_far, owner == outer))
+        entries.append((owner, loc, is_far, is_middle, middle_seen))
+        middle_seen = middle_seen + jnp.where(is_middle, one, zero)
+        for l in range(OWN):
+            needed[l] = jnp.where(jnp.logical_and(is_far, loc == l), one, needed[l])
+    free_rank = []
+    seen = zero
+    for l in range(OWN):
+        free_rank.append(jnp.where(needed[l] == 0, seen, jnp.int32(-1)))
+        seen = seen + (one - needed[l])
+    for n, (owner, loc, is_far, is_middle, rank_n) in enumerate(entries):
+        slot = zero
+        for l in range(OWN):
+            slot = jnp.where(free_rank[l] == rank_n - EARLY, jnp.int32(l), slot)
+        row = jnp.where(is_middle, jnp.where(rank_n < EARLY, rank_n, 8 + slot), jnp.where(is_far, 8 + loc, 4 + loc))
+        owner_z, loc_z = owner_of(source[n // OWN, z * OWN + n % OWN])
+        at_inner = jnp.where(
+            owner_z == z, 4 + loc_z, jnp.where(owner_z == peer, loc_z, jnp.where(owner_z == near, 12 + loc_z, 8 + loc_z))
+        )
+        picks[n] = jnp.where(is_inner, at_inner, row)
+    for e in range(2 * EARLY):
+        pick = zero if e < EARLY else jnp.where(needed[e - EARLY] == 1, jnp.int32(8 + e - EARLY), zero)
+        for owner, loc, is_far, is_middle, rank_n in entries:
+            mine = rank_n == e if e < EARLY else rank_n - EARLY == free_rank[e - EARLY]
+            mine = jnp.logical_and(mine, is_middle)
+            if e >= EARLY:
+                mine = jnp.logical_and(mine, needed[e - EARLY] == 0)
+            pick = jnp.where(mine, jnp.where(owner == z, 4 + loc, loc), pick)
+        picks[HOPS * OWN + e] = pick
+
+    def exchange(k, meanwhile):
+        for i in range(CHUNKS + RELAY_LAG + LATE_LAG):
+
+            @pl.when(is_inner)
+            def _():
+                if i < CHUNKS:
+                    to_peer(k, i).wait_recv()
+                    for e in range(EARLY):
+                        early_bufs[k][i, e] = near_bufs[k][i][picks[HOPS * OWN + e]]
+                    early(k, i).start()
+                c = i - RELAY_LAG
+                if 0 <= c < CHUNKS:
+                    to_near(k, c).wait_recv()
+                    relay(k, c).start()
+                c -= LATE_LAG
+                if c >= 0:
+                    relay(k, c).wait_recv()
+                    for e in range(EARLY):
+                        late_bufs[k][c, e] = chunk_of(k, c, picks[HOPS * OWN + EARLY + e])
+                    late(k, c).start()
+
+            if i < OWN:
+                meanwhile(i)
+
+        @pl.when(is_outer)
+        def _():
             for c in range(CHUNKS):
-                to_peer(k, c).wait_recv()
-                to_far(k, c).wait_recv()
-                to_near(k, c).wait_recv()
-                for s, pick in enumerate(picks):
-                    packed[k][c, s] = chunk_bufs[k][c][pick]
-                to_outer(k, c).start()
-
-        @pl.when(is_outer)
-        def _():
-            for c in range(CHUNKS):
-                to_outer(k, c).wait_recv()
-
-    def picked(b, j):
-        owner, loc = owner_of(source[b, z * OWN + j])
-        at_inner = jnp.where(
-            owner == peer, loc, jnp.where(owner == far, 4 + loc, jnp.where(owner == near, 8 + loc, 12 + loc))
-        )
-        at_outer = jnp.where(owner == z, 12 + loc, b * OWN + j)
-        return jnp.where(is_inner, at_inner, at_outer)
+                early(k, c).wait_recv()
+                late(k, c).wait_recv()
+
+    def picked(k, b, j):
+        i = picks[b * OWN + j]
+        return jnp.concatenate([chunk_of(k, c, i) for c in range(CHUNKS)], axis=0)
 
     def dot(a, b):
         return jnp.dot(a, b, preferred_element_type=f32)
@@ -174,7 +224,7 @@
         gram_acc[entry(0, 0)] += pair_dot(value, value)
         return carry
 
-    lax.fori_loop(0, OWN, first, 0)
+    lax.fori_loop(0, OWN, first, 0, unroll=True)
     pl.semaphore_wait(barrier, 5)
     send_own(0)
     for copy in loads[1:]:
@@ -182,24 +232,18 @@
 
     for k in range(STEPS):
 
-        def on_site(j, carry):
-            own = block(k, 12 + j)
-            total = None
-            for a in range(2):
-                half = dot(left[a, j], own).astype(bf16)
-                term = dot(half, right[a, j])
-                total = term if total is None else total + term
-            vec[k + 1][j] = total
-            return carry
-
-        lax.fori_loop(0, OWN, on_site, 0)
-        exchange(k)
+        def on_site(j):
+            half = dot(left[:, j].reshape(2 * blk, blk), own_block(k, j)).astype(bf16)
+            both = jnp.concatenate([half[:blk], half[blk:]], axis=1)
+            vec[k + 1][j] = dot(both, right[:, j].reshape(2 * blk, blk))
+
+        exchange(k, on_site)
 
         def hop(j, carry):
-            total = vec[k + 1][j]
-            for b in range(2):
-                half = dot(hop_left[b, j], block(k, picked(b, j))).astype(bf16)
-                total = total + dot(half, hop_right[b, j])
+            both = jnp.concatenate(
+                [dot(hop_left[b, j], picked(k, b, j)).astype(bf16) for b in range(HOPS)], axis=1
+            )
+            total = vec[k + 1][j] + dot(both, hop_right[:, j].reshape(2 * blk, blk))
             total = kept(j, total)
             vec[k + 1][j] = total
             if k + 1 < STEPS:
@@ -209,7 +253,7 @@
                 gram_acc[entry(i, k + 1)] += pair_dot(total, other)
             return carry
 
-        lax.fori_loop(0, OWN, hop, 0)
+        lax.fori_loop(0, OWN, hop, 0, unroll=True)
         if k + 1 < STEPS:
             send_own(k + 1)
 
@@ -278,7 +322,7 @@
 
         return carry
 
-    lax.fori_loop(0, OWN, finish, 0)
+    lax.fori_loop(0, OWN, finish, 0, unroll=True)
     put_state = pltpu.make_async_copy(final, state_out.at[0], out_sem)
     put_state.start()
 
@@ -287,14 +331,15 @@
         @pl.when(is_outer)
         def _():
             for c in range(CHUNKS):
-                to_far(k, c).wait_send()
                 to_near(k, c).wait_send()
 
         @pl.when(is_inner)
         def _():
             for c in range(CHUNKS):
                 to_peer(k, c).wait_send()
-                to_outer(k, c).wait_send()
+                relay(k, c).wait_send()
+                early(k, c).wait_send()
+                late(k, c).wait_send()
 
     for d in range(1, 4):
         gram_copy(d).wait_send()
@@ -334,8 +379,8 @@
         in_specs=[smem] * 3 + [hbm] * 5,
         out_specs=(hbm, hbm, hbm),
         scratch_shapes=[
-            *[pltpu.VMEM((16, rows, blk), bf16) for _ in range(STEPS * CHUNKS)],
-            *[pltpu.VMEM((CHUNKS, SLOTS, rows, blk), bf16) for _ in range(STEPS)],
+            *[pltpu.VMEM((8, rows, blk), bf16) for _ in range(2 * STEPS * CHUNKS)],
+            *[pltpu.VMEM((CHUNKS, EARLY, rows, blk), bf16) for _ in range(2 * STEPS)],
             *[pltpu.VMEM((own, blk, blk), f32) for _ in range(STEPS + 1)],
             pltpu.VMEM((own, blk, blk), f32),
             *[pltpu.VMEM(env, bf16) for _ in range(4)],
@@ -345,9 +390,10 @@
             pltpu.VMEM((len(ENTRIES), 8, blk), f32),
             pltpu.VMEM((3, 16, 128), f32),
             pltpu.VMEM((16, 128), f32),
+            pltpu.SMEM((HOPS * OWN + 2 * EARLY,), jnp.int32),
             dma((5,)),
             dma((STEPS, CHUNKS, 4)),
-            dma((STEPS, CHUNKS, 4)),
+            dma((STEPS, CHUNKS, 3)),
             dma((3,)),
             dma((3,)),
             dma((2, 2, own)),
@@ -355,7 +401,7 @@
             dma,
         ],
         compiler_params=pltpu.CompilerParams(
-            collective_id=0, has_side_effects=True, vmem_limit_bytes=48 * 1024 * 1024
+            collective_id=0, has_side_effects=True, vmem_limit_bytes=67_000_000
         ),
     )(kept_rank, step_size, hop_source, psi, left_env, right_env, hop_left, hop_right)
     me_c = lax.axis_index("chain")

time: 167 us -> 145 us (0.87)
  Pallas kernels: 157 us -> 136 us
  local copies, waits for them, and re-layouts: 5.4 us -> 0.97 us
  other arithmetic: 2.67 us -> 4.91 us
    pallas_call x1, Pallas kernels: 157 us -> 136 us  [on_device(): pl.pallas_call(kernel, out_shape=(jax.ShapeDtypeStruct(psi.shape, f32), j...]
    unnamed x13 -> x3, local copies, waits for them, and re-layouts: 5.4 us -> 0.97 us
    broadcast_in_dim x1, other arithmetic: 2.67 us -> 4.91 us  [on_device(): return (state, merged_left[None], merged_right[None])]
where the time goes in v2:
time: 145 us; the launch traced here: 143 us
  Pallas kernels  136 us (94%)
  other arithmetic  4.91 us (3%)
    pallas_call x1, Pallas kernels, on_device(): pl.pallas_call(kernel, out_shape=(jax.ShapeDtypeStruct(psi.shape, f32), j...  136 us
    broadcast_in_dim x1, other arithmetic, on_device(): return (state, merged_left[None], merged_right[None])  4.91 us

profile of v2, /device:TPU:40, one launch (start us, length us, event | category | flops | bytes accessed | tf_op | source)
XLA Modules:
  0.0 142.8 jit_solution(12452855021676179974)
XLA Ops:
  0.6 136.3 %shard_map.103 = (f32[1,4,256,256]{3,2,1,0:T(8,128)}, bf16[2,4,256,256]{3,2,1,0:T(8,128)(2,1)}, bf16[2,4,256,256]{3,2,1,0:T(8,128)(2,1)}) custom-call(s32[1,4]{1,0:T(1,128)} %rank.1, f32[1,3]{1,0:T(1,128)} %step_size.1, s32[2,16]{1,0:T(2,128)} %source.1, f32[1,4,256,256]{3,2,1,0:T(8,128)} %psi_hbm.1, bf16[1,2,4,256,256]{4,3,2,1,0:T(8,128)(2,1)} %left_hbm.1, ...), custom_call_target="tpu_custom_call" | custom-call | tf_op jit(solution)/shard_map/pallas_call | solution.py:372
  136.9 0.0 copy-start
  137.0 4.9 %fusion = (f32[1,2,4,256,256]{4,3,2,1,0:T(8,128)}, f32[1,2,4,256,256]{4,3,2,1,0:T(8,128)}) fusion(bf16[2,4,256,256]{3,2,1,0:T(8,128)(2,1)} %get-tuple-element.8, bf16[1,2,4,256,256]{4,3,2,1,0:T(8,128)(2,1)} %right_hbm.1, pred[]{:T(512)S(6)} %eq.7, bf16[2,4,256,256]{3,2,1,0:T(8,128)(2,1)} %get-tuple-element.7, pred[]{:T(512)S(6)} %eq.6, ...), kind=kLoop, calls=%fused_computation.1 | loop fusion | flops 4194304 | bytes 8388610 | tf_op jit(solution)/shard_map/broadcast_in_dim | solution.py:411
  141.9 0.0 copy-done
  141.9 1.0 copy.12
Async XLA Ops:
  136.9 4.9 %copy-start = (f32[1,4,256,256]{3,2,1,0:T(8,128)S(1)}, f32[1,4,256,256]{3,2,1,0:T(8,128)}, u32[]{:S(2)}) copy-start(f32[1,4,256,256]{3,2,1,0:T(8,128)} %get-tuple-element.14) | copy-start | bytes 3145732

commit v3 on v2

--- a/solution.py
+++ b/solution.py
@@ -37,7 +37,7 @@
 def kernel(
     rank, step_size, source,
     psi_hbm, left_hbm, right_hbm, hop_left_hbm, hop_right_hbm,
-    state_out, from_left, from_right,
+    final, merged_left, merged_right,
     *scratch,
 ):
     f32, bf16 = jnp.float32, jnp.bfloat16
@@ -50,8 +50,8 @@
     at += 2 * STEPS
     vec = scratch[at : at + STEPS + 1]
     at += STEPS + 1
-    (psi, left, right, hop_left, hop_right, final, send_left, send_right, gram_acc, gram_in, gram_out, picks,
-     load_sem, send_sem, recv_sem, gram_send, gram_recv, merge_send, merge_recv, out_sem) = scratch[at:]
+    (psi, left, right, hop_left, hop_right, send_left, send_right, from_left, from_right, gram_acc, gram_in, gram_out, picks,
+     load_sem, send_sem, recv_sem, gram_send, gram_recv, merge_send, merge_recv) = scratch[at:]
 
     me_c = lax.axis_index("chain")
     n_c = lax.axis_size("chain")
@@ -80,8 +80,17 @@
     barrier = pltpu.get_barrier_semaphore()
     for d in range(1, 4):
         pl.semaphore_signal(barrier, inc=1, device_id=(me_c, lax.rem(z + d, 4)), device_id_type=MESH)
-    for c in (prv, nxt):
-        pl.semaphore_signal(barrier, inc=1, device_id=(c, z), device_id_type=MESH)
+    has_next = me_c < n_c - 1
+    has_prev = me_c > 0
+
+    @pl.when(has_prev)
+    def _():
+        pl.semaphore_signal(barrier, inc=1, device_id=(prv, z), device_id_type=MESH)
+
+    @pl.when(has_next)
+    def _():
+        pl.semaphore_signal(barrier, inc=1, device_id=(nxt, z), device_id_type=MESH)
+
 
     row_at = lax.broadcasted_iota(jnp.int32, (blk, blk), 0)
     col_at = lax.broadcasted_iota(jnp.int32, (blk, blk), 1)
@@ -225,7 +234,7 @@
         return carry
 
     lax.fori_loop(0, OWN, first, 0, unroll=True)
-    pl.semaphore_wait(barrier, 5)
+    pl.semaphore_wait(barrier, jnp.where(jnp.logical_and(has_prev, has_next), 5, 4))
     send_own(0)
     for copy in loads[1:]:
         copy.wait()
@@ -294,14 +303,11 @@
             recv_sem=merge_recv.at[direction, a, j], device_id=(to, z), device_id_type=MESH,
         )
 
-    has_next = me_c < n_c - 1
-    has_prev = me_c > 0
-
     def finish(j, carry):
         value = coef[0] * vec[0][j]
         for i in range(1, STEPS + 1):
             value = value + coef[i] * vec[i][j]
-        final[j] = value
+        final[0, j] = value
         own = value.astype(bf16)
         own_t = value.T.astype(bf16)
         for a in range(2):
@@ -323,8 +329,29 @@
         return carry
 
     lax.fori_loop(0, OWN, finish, 0, unroll=True)
-    put_state = pltpu.make_async_copy(final, state_out.at[0], out_sem)
-    put_state.start()
+    def receive(direction, a, j, out, env, got):
+        merge(direction, a, j).wait_recv()
+        out[0, a, j] = env[a, j].astype(f32) + got[a, j].astype(f32)
+
+    @pl.when(has_prev)
+    def _():
+        for j in range(OWN):
+            for a in range(2):
+                receive(0, a, j, merged_left, left, from_left)
+
+    @pl.when(has_next)
+    def _():
+        for j in range(OWN):
+            for a in range(2):
+                receive(1, a, j, merged_right, right, from_right)
+
+    @pl.when(jnp.logical_not(has_prev))
+    def _():
+        merged_left[0] = left[...].astype(f32)
+
+    @pl.when(jnp.logical_not(has_next))
+    def _():
+        merged_right[0] = right[...].astype(f32)
 
     for k in range(STEPS):
 
@@ -349,16 +376,25 @@
         for a in range(2):
             for j in range(OWN):
                 merge(0, a, j).wait_send()
-                merge(1, a, j).wait_recv()
 
     @pl.when(has_prev)
     def _():
         for a in range(2):
             for j in range(OWN):
                 merge(1, a, j).wait_send()
-                merge(0, a, j).wait_recv()
-
-    put_state.wait()
+
+
+def write_out(*refs):
+    count = (len(refs) - 1) // 2
+    copies = [
+        pltpu.make_async_copy(refs[i].at[0, j], refs[count + i].at[0, j], refs[-1].at[i, j])
+        for i in range(count)
+        for j in range(refs[i].shape[1])
+    ]
+    for copy in copies:
+        copy.start()
+    for copy in copies:
+        copy.wait()
 
 
 def on_device(psi, kept_rank, step_size, left_env, right_env, hop_left, hop_right, hop_source):
@@ -369,24 +405,20 @@
     smem = pl.BlockSpec(memory_space=pltpu.SMEM)
     hbm = pl.BlockSpec(memory_space=pl.ANY)
     dma = pltpu.SemaphoreType.DMA
-    state, from_left, from_right = pl.pallas_call(
+    shapes = (psi.shape, left_env.shape, right_env.shape)
+    held = [pltpu.with_memory_space_constraint(x, pltpu.HBM) for x in (psi, left_env, right_env, hop_left, hop_right)]
+    results = pl.pallas_call(
         kernel,
-        out_shape=(
-            jax.ShapeDtypeStruct(psi.shape, f32),
-            jax.ShapeDtypeStruct(env, bf16),
-            jax.ShapeDtypeStruct(env, bf16),
-        ),
+        out_shape=tuple(pltpu.VMEM(shape, f32) for shape in shapes),
         in_specs=[smem] * 3 + [hbm] * 5,
-        out_specs=(hbm, hbm, hbm),
+        out_specs=(pl.BlockSpec(memory_space=pltpu.VMEM),) * 3,
         scratch_shapes=[
             *[pltpu.VMEM((8, rows, blk), bf16) for _ in range(2 * STEPS * CHUNKS)],
             *[pltpu.VMEM((CHUNKS, EARLY, rows, blk), bf16) for _ in range(2 * STEPS)],
             *[pltpu.VMEM((own, blk, blk), f32) for _ in range(STEPS + 1)],
             pltpu.VMEM((own, blk, blk), f32),
             *[pltpu.VMEM(env, bf16) for _ in range(4)],
-            pltpu.VMEM((own, blk, blk), f32),
-            pltpu.VMEM(env, bf16),
-            pltpu.VMEM(env, bf16),
+            *[pltpu.VMEM(env, bf16) for _ in range(4)],
             pltpu.VMEM((len(ENTRIES), 8, blk), f32),
             pltpu.VMEM((3, 16, 128), f32),
             pltpu.VMEM((16, 128), f32),
@@ -398,17 +430,19 @@
             dma((3,)),
             dma((2, 2, own)),
             dma((2, 2, own)),
-            dma,
         ],
         compiler_params=pltpu.CompilerParams(
-            collective_id=0, has_side_effects=True, vmem_limit_bytes=67_000_000
+            collective_id=0, has_side_effects=True, vmem_limit_bytes=61_700_000
         ),
-    )(kept_rank, step_size, hop_source, psi, left_env, right_env, hop_left, hop_right)
-    me_c = lax.axis_index("chain")
-    last = lax.axis_size("chain") - 1
-    merged_left = left_env[0].astype(f32) + jnp.where(me_c == 0, 0.0, from_left.astype(f32))
-    merged_right = right_env[0].astype(f32) + jnp.where(me_c == last, 0.0, from_right.astype(f32))
-    return state, merged_left[None], merged_right[None]
+    )(kept_rank, step_size, hop_source, *held)
+    return pl.pallas_call(
+        write_out,
+        out_shape=tuple(jax.ShapeDtypeStruct(shape, f32) for shape in shapes),
+        in_specs=[pl.BlockSpec(memory_space=pltpu.VMEM)] * 3,
+        out_specs=(hbm,) * 3,
+        scratch_shapes=[dma((3, own))],
+        compiler_params=pltpu.CompilerParams(vmem_limit_bytes=8 * 1024 * 1024),
+    )(*[pltpu.with_memory_space_constraint(x, pltpu.VMEM) for x in results])
 
 
 def solution(mesh):

time: 145 us -> 141 us (0.972)
  other arithmetic: 4.91 us -> 0 us
  Pallas kernels: 136 us -> 139 us
    broadcast_in_dim x1 -> x0, other arithmetic: 4.91 us -> none  [on_device(): return (state, merged_left[None], merged_right[None])]
    pallas_call x1 -> x2, Pallas kernels: 136 us -> 139 us  [the longest x1 136 us: on_device(): pl.pallas_call(kernel, out_shape=tuple((pltpu.VMEM(shape, f32) for shape...]
where the time goes in v3:
time: 141 us; the launch traced here: 139 us
  Pallas kernels  139 us (99%)
    pallas_call x1, Pallas kernels, on_device(): pl.pallas_call(kernel, out_shape=tuple((pltpu.VMEM(shape, f32) for shape...  136 us

profile of v3, /device:TPU:40, one launch (start us, length us, event | category | flops | bytes accessed | tf_op | source)
XLA Modules:
  0.0 139.4 jit_solution(10859720766212164798)
XLA Ops:
  0.6 136.3 %shard_map.103 = (f32[1,4,256,256]{3,2,1,0:T(8,128)S(1)}, f32[1,2,4,256,256]{4,3,2,1,0:T(8,128)S(1)}, f32[1,2,4,256,256]{4,3,2,1,0:T(8,128)S(1)}) custom-call(s32[1,4]{1,0:T(1,128)} %rank.1, f32[1,3]{1,0:T(1,128)} %step_size.1, s32[2,16]{1,0:T(2,128)} %source.1, f32[1,4,256,256]{3,2,1,0:T(8,128)} %psi_hbm.1, bf16[1,2,4,256,256]{4,3,2,1,0:T(8,128)(2,1)} %left_hbm.1, ...), custom_call_target="tpu_custom_call" | custom-call | tf_op jit(solution)/shard_map/pallas_call | solution.py:410
  136.9 2.5 %shard_map.104 = (f32[1,4,256,256]{3,2,1,0:T(8,128)}, f32[1,2,4,256,256]{4,3,2,1,0:T(8,128)}, f32[1,2,4,256,256]{4,3,2,1,0:T(8,128)}) custom-call(f32[1,4,256,256]{3,2,1,0:T(8,128)S(1)} %get-tuple-element.6.refs_0_, f32[1,2,4,256,256]{4,3,2,1,0:T(8,128)S(1)} %get-tuple-element.7.refs_1_, f32[1,2,4,256,256]{4,3,2,1,0:T(8,128)S(1)} %get-tuple-element.8.refs_2_), custom_call_target="tpu_custom_call" | custom-call | tf_op jit(solution)/shard_map/pallas_call | solution.py:438

commit v4 on v3

--- a/solution.py
+++ b/solution.py
@@ -1,3 +1,5 @@
+import functools
+
 import jax
 import jax.numpy as jnp
 from jax import lax
@@ -9,7 +11,8 @@
 STEPS = 3
 OWN = 4
 HOPS = 2
-EARLY = 4
+LATE = 4
+SIZES = (8, 7, 6)
 CHUNKS = 8
 RELAY_LAG = CHUNKS - 2
 LATE_LAG = 2
@@ -34,20 +37,46 @@
     return total
 
 
+def plan_kernel(source, plan, choice):
+    need = []
+    for d in range(4):
+        mask = jnp.int32(0)
+        for n in range(HOPS * OWN):
+            mask = mask | (jnp.int32(1) << source[n // OWN, d * OWN + n % OWN])
+        need.append(mask)
+        plan[d] = mask
+
+    def count(mask):
+        mask = mask - ((mask >> 1) & 0x5555)
+        mask = (mask & 0x3333) + ((mask >> 2) & 0x3333)
+        mask = (mask + (mask >> 4)) & 0x0F0F
+        return (mask + (mask >> 8)) & 0x1F
+
+    most = count((need[2] | need[3]) & 0x00FF)
+    for mask in ((need[0] | need[1]) & 0xFF00, need[3] & 0x0FFF, need[0] & 0xFFF0):
+        most = jnp.maximum(most, count(mask))
+    index = jnp.int32(0)
+    for i, size in enumerate(SIZES):
+        index = jnp.where(most <= size, jnp.int32(i), index)
+    choice[0] = index
+
+
 def kernel(
-    rank, step_size, source,
+    size, rank, step_size, source, plan,
     psi_hbm, left_hbm, right_hbm, hop_left_hbm, hop_right_hbm,
     final, merged_left, merged_right,
     *scratch,
 ):
     f32, bf16 = jnp.float32, jnp.bfloat16
     per = STEPS * CHUNKS
-    near_bufs = [scratch[k * CHUNKS : (k + 1) * CHUNKS] for k in range(STEPS)]
-    far_bufs = [scratch[per + k * CHUNKS : per + (k + 1) * CHUNKS] for k in range(STEPS)]
-    at = 2 * per
-    early_bufs = scratch[at : at + STEPS]
-    late_bufs = scratch[at + STEPS : at + 2 * STEPS]
-    at += 2 * STEPS
+    near_bufs, late_bufs, outer_bufs = (
+        [scratch[(i * STEPS + k) * CHUNKS : (i * STEPS + k + 1) * CHUNKS] for k in range(STEPS)] for i in range(3)
+    )
+    at = 3 * per
+    mid_early, mid_late, out_early, out_late = (scratch[at + i * STEPS : at + (i + 1) * STEPS] for i in range(4))
+    at += 4 * STEPS
+    first_part = size - LATE
+    direct = first_part == OWN
     vec = scratch[at : at + STEPS + 1]
     at += STEPS + 1
     (psi, left, right, hop_left, hop_right, send_left, send_right, from_left, from_right, gram_acc, gram_in, gram_out, picks,
@@ -74,8 +103,7 @@
         pltpu.make_async_copy(hop_left_hbm.at[0], hop_left, load_sem.at[3]),
         pltpu.make_async_copy(hop_right_hbm.at[0], hop_right, load_sem.at[4]),
     ]
-    for copy in loads:
-        copy.start()
+    loads[0].start()
 
     barrier = pltpu.get_barrier_semaphore()
     for d in range(1, 4):
@@ -102,15 +130,23 @@
     def put_own(k, j, value):
         value = value.astype(bf16)
         for c in range(CHUNKS):
-            near_bufs[k][c][4 + j] = value[c * rows : (c + 1) * rows]
+            part = value[c * rows : (c + 1) * rows]
+            near_bufs[k][c][4 + j] = part
+            if not direct:
+                for e in range(first_part):
+                    mid_early[k][c, e] = part if j == 0 else jnp.where(picks[16 + e] == j, part, mid_early[k][c, e])
 
     def own_block(k, j):
         return jnp.concatenate([near_bufs[k][c][4 + j] for c in range(CHUNKS)], axis=0)
 
     def chunk_of(k, c, i):
-        return jnp.where(
-            i < 8, near_bufs[k][c][jnp.minimum(i, 7)], far_bufs[k][c][jnp.maximum(i - 8, 0)]
+        got = jnp.where(
+            i < 8, near_bufs[k][c][jnp.minimum(i, 7)], late_bufs[k][c][jnp.minimum(jnp.maximum(i - 8, 0), 3)]
         )
+        return jnp.where(i < 12, got, outer_bufs[k][c][jnp.maximum(i - 12, 0)])
+
+    def near_or(k, c, i, other, start):
+        return jnp.where(i < 8, near_bufs[k][c][jnp.minimum(i, 7)], other[k][c][jnp.maximum(i - start, 0)])
 
     def remote(src, dst, k, c, sent, received, to):
         return pltpu.make_async_remote_copy(
@@ -118,20 +154,24 @@
             device_id=(me_c, to), device_id_type=MESH,
         )
 
+    def arrive(k, c, late):
+        return late_bufs[k][c] if late else near_bufs[k][c].at[0:first_part]
+
     def to_peer(k, c):
-        return remote(near_bufs[k][c].at[4:8], near_bufs[k][c].at[0:4], k, c, 0, 0, peer)
+        src = near_bufs[k][c].at[4:8] if direct else mid_early[k].at[c]
+        return remote(src, arrive(k, c, False), k, c, 0, 0, peer)
 
     def to_near(k, c):
-        return remote(near_bufs[k][c].at[4:8], far_bufs[k][c].at[4:8], k, c, 0, 2, near)
+        return remote(near_bufs[k][c].at[4:8], outer_bufs[k][c], k, c, 0, 2, near)
 
     def relay(k, c):
-        return remote(far_bufs[k][c].at[4:8], far_bufs[k][c].at[0:4], k, c, 1, 1, peer)
+        return remote(mid_late[k].at[c], arrive(k, c, True), k, c, 1, 1, peer)
 
     def early(k, c):
-        return remote(early_bufs[k].at[c], near_bufs[k][c].at[0:4], k, c, 2, 0, near)
+        return remote(out_early[k].at[c], arrive(k, c, False), k, c, 2, 0, near)
 
     def late(k, c):
-        return remote(late_bufs[k].at[c], far_bufs[k][c].at[0:4], k, c, 3, 1, near)
+        return remote(out_late[k].at[c], arrive(k, c, True), k, c, 3, 1, near)
 
     def send_own(k):
         @pl.when(is_outer)
@@ -144,47 +184,72 @@
             for c in range(CHUNKS):
                 to_peer(k, c).start()
 
-    def owner_of(s):
-        owner = s // OWN
-        return owner, s - owner * OWN
-
-    outer = jnp.where(is_inner, near, z)
     zero, one = jnp.int32(0), jnp.int32(1)
-    middle_seen = zero
-    needed = [zero] * OWN
-    entries = []
-    for n in range(HOPS * OWN):
-        owner, loc = owner_of(source[n // OWN, outer * OWN + n % OWN])
-        is_far = owner == 3 - outer
-        is_middle = jnp.logical_not(jnp.logical_or(is_far, owner == outer))
-        entries.append((owner, loc, is_far, is_middle, middle_seen))
-        middle_seen = middle_seen + jnp.where(is_middle, one, zero)
-        for l in range(OWN):
-            needed[l] = jnp.where(jnp.logical_and(is_far, loc == l), one, needed[l])
-    free_rank = []
-    seen = zero
+    x = jnp.where(is_inner, z, near)
+    y = 3 - x
+    o = x + 1 - 2 * lax.rem(x, 2)
+    yo = 3 - o
+
+    def bits(mask, device):
+        return [(mask >> (OWN * device + l)) & 1 for l in range(OWN)]
+
+    def to_middle(a, ao, b, bo):
+        mask = plan[b] | plan[bo]
+        theirs, seen = [], zero
+        for l, bit in enumerate(bits(mask, ao)):
+            theirs.append((bit, 8 + seen, jnp.int32(12 + l)))
+            seen = seen + bit
+        mine, rank_l = [], zero
+        for l, bit in enumerate(bits(mask, a)):
+            if direct:
+                mine.append((bit, jnp.int32(l), jnp.int32(4 + l)))
+            else:
+                row = jnp.where(rank_l < first_part, rank_l, 8 + seen + rank_l - first_part)
+                mine.append((bit, row, jnp.int32(4 + l)))
+                rank_l = rank_l + bit
+        return mine, theirs
+
+    sent_own, sent_outer = to_middle(x, o, y, yo)
+    got_own, got_outer = to_middle(y, yo, x, o)
+
+    def choose(items, row):
+        pick = zero
+        for bit, at_b, code in items:
+            pick = jnp.where(jnp.logical_and(bit == 1, at_b == row), code, pick)
+        return pick
+
+    mask = plan[o]
+    ready, seen, late_seen = [], zero, zero
+    held = []
+    for l, bit in enumerate(bits(mask, yo)):
+        held.append((bit, 8 + late_seen, got_outer[l][1]))
+        late_seen = late_seen + bit
+    middle_late = []
+    for l, bit in enumerate(bits(mask, y)):
+        is_late = jnp.where(got_own[l][1] >= 8, bit, zero)
+        middle_late.append((is_late, 8 + late_seen, got_own[l][1]))
+        late_seen = late_seen + is_late
+    for l, bit in enumerate(bits(mask, x)):
+        ready.append((bit, seen, jnp.int32(4 + l)))
+        seen = seen + bit
+    for l, bit in enumerate(bits(mask, y)):
+        is_early = jnp.where(got_own[l][1] < 8, bit, zero)
+        ready.append((is_early, seen, got_own[l][1]))
+        seen = seen + is_early
+    ready = [
+        (bit, jnp.where(at < first_part, at, 8 + late_seen + at - first_part), code) for bit, at, code in ready
+    ]
     for l in range(OWN):
-        free_rank.append(jnp.where(needed[l] == 0, seen, jnp.int32(-1)))
-        seen = seen + (one - needed[l])
-    for n, (owner, loc, is_far, is_middle, rank_n) in enumerate(entries):
-        slot = zero
-        for l in range(OWN):
-            slot = jnp.where(free_rank[l] == rank_n - EARLY, jnp.int32(l), slot)
-        row = jnp.where(is_middle, jnp.where(rank_n < EARLY, rank_n, 8 + slot), jnp.where(is_far, 8 + loc, 4 + loc))
-        owner_z, loc_z = owner_of(source[n // OWN, z * OWN + n % OWN])
-        at_inner = jnp.where(
-            owner_z == z, 4 + loc_z, jnp.where(owner_z == peer, loc_z, jnp.where(owner_z == near, 12 + loc_z, 8 + loc_z))
-        )
-        picks[n] = jnp.where(is_inner, at_inner, row)
-    for e in range(2 * EARLY):
-        pick = zero if e < EARLY else jnp.where(needed[e - EARLY] == 1, jnp.int32(8 + e - EARLY), zero)
-        for owner, loc, is_far, is_middle, rank_n in entries:
-            mine = rank_n == e if e < EARLY else rank_n - EARLY == free_rank[e - EARLY]
-            mine = jnp.logical_and(mine, is_middle)
-            if e >= EARLY:
-                mine = jnp.logical_and(mine, needed[e - EARLY] == 0)
-            pick = jnp.where(mine, jnp.where(owner == z, 4 + loc, loc), pick)
-        picks[HOPS * OWN + e] = pick
+        picks[OWN * z + l] = jnp.int32(4 + l)
+        picks[OWN * near + l] = jnp.where(is_inner, jnp.int32(12 + l), ready[l][1])
+        at_o = jnp.where(middle_late[l][0] == 1, middle_late[l][1], ready[OWN + l][1])
+        picks[OWN * y + l] = jnp.where(is_inner, got_own[l][1], at_o)
+        picks[OWN * yo + l] = jnp.where(is_inner, got_outer[l][1], held[l][1])
+    for e in range(OWN):
+        picks[16 + e] = choose(sent_own, e) - 4
+        picks[20 + e] = choose([*sent_own, *sent_outer], 8 + e)
+        picks[24 + e] = choose(ready, e)
+        picks[28 + e] = choose([*held, *middle_late, *ready], 8 + e)
 
     def exchange(k, meanwhile):
         for i in range(CHUNKS + RELAY_LAG + LATE_LAG):
@@ -193,18 +258,20 @@
             def _():
                 if i < CHUNKS:
                     to_peer(k, i).wait_recv()
-                    for e in range(EARLY):
-                        early_bufs[k][i, e] = near_bufs[k][i][picks[HOPS * OWN + e]]
+                    for e in range(first_part):
+                        out_early[k][i, e] = near_bufs[k][i][picks[24 + e]]
                     early(k, i).start()
                 c = i - RELAY_LAG
                 if 0 <= c < CHUNKS:
                     to_near(k, c).wait_recv()
+                    for e in range(LATE):
+                        mid_late[k][c, e] = near_or(k, c, picks[20 + e], outer_bufs, 12)
                     relay(k, c).start()
                 c -= LATE_LAG
                 if c >= 0:
                     relay(k, c).wait_recv()
-                    for e in range(EARLY):
-                        late_bufs[k][c, e] = chunk_of(k, c, picks[HOPS * OWN + EARLY + e])
+                    for e in range(LATE):
+                        out_late[k][c, e] = near_or(k, c, picks[28 + e], late_bufs, 8)
                     late(k, c).start()
 
             if i < OWN:
@@ -217,7 +284,7 @@
                 late(k, c).wait_recv()
 
     def picked(k, b, j):
-        i = picks[b * OWN + j]
+        i = picks[source[b, z * OWN + j]]
         return jnp.concatenate([chunk_of(k, c, i) for c in range(CHUNKS)], axis=0)
 
     def dot(a, b):
@@ -225,18 +292,18 @@
 
     gram_acc[...] = jnp.zeros_like(gram_acc)
     loads[0].wait()
-
-    def first(j, carry):
+    for copy in loads[1:]:
+        copy.start()
+
+    for j in range(OWN):
         value = kept(j, psi[j])
         vec[0][j] = value
         put_own(0, j, value)
         gram_acc[entry(0, 0)] += pair_dot(value, value)
-        return carry
-
-    lax.fori_loop(0, OWN, first, 0, unroll=True)
+
     pl.semaphore_wait(barrier, jnp.where(jnp.logical_and(has_prev, has_next), 5, 4))
     send_own(0)
-    for copy in loads[1:]:
+    for copy in loads[1:3]:
         copy.wait()
 
     for k in range(STEPS):
@@ -247,8 +314,11 @@
             vec[k + 1][j] = dot(both, right[:, j].reshape(2 * blk, blk))
 
         exchange(k, on_site)
-
-        def hop(j, carry):
+        if k == 0:
+            for copy in loads[3:]:
+                copy.wait()
+
+        for j in range(OWN):
             both = jnp.concatenate(
                 [dot(hop_left[b, j], picked(k, b, j)).astype(bf16) for b in range(HOPS)], axis=1
             )
@@ -260,9 +330,6 @@
             for i in range(k + 2):
                 other = total if i == k + 1 else vec[i][j]
                 gram_acc[entry(i, k + 1)] += pair_dot(total, other)
-            return carry
-
-        lax.fori_loop(0, OWN, hop, 0, unroll=True)
         if k + 1 < STEPS:
             send_own(k + 1)
 
@@ -397,7 +464,8 @@
         copy.wait()
 
 
-def on_device(psi, kept_rank, step_size, left_env, right_env, hop_left, hop_right, hop_source):
+def window(index, plan, psi, kept_rank, step_size, left_env, right_env, hop_left, hop_right, hop_source):
+    size = SIZES[index]
     f32, bf16 = jnp.float32, jnp.bfloat16
     own, blk = psi.shape[1], psi.shape[2]
     rows = blk // CHUNKS
@@ -408,13 +476,18 @@
     shapes = (psi.shape, left_env.shape, right_env.shape)
     held = [pltpu.with_memory_space_constraint(x, pltpu.HBM) for x in (psi, left_env, right_env, hop_left, hop_right)]
     results = pl.pallas_call(
-        kernel,
+        functools.partial(kernel, size),
         out_shape=tuple(pltpu.VMEM(shape, f32) for shape in shapes),
-        in_specs=[smem] * 3 + [hbm] * 5,
+        in_specs=[smem] * 4 + [hbm] * 5,
         out_specs=(pl.BlockSpec(memory_space=pltpu.VMEM),) * 3,
         scratch_shapes=[
-            *[pltpu.VMEM((8, rows, blk), bf16) for _ in range(2 * STEPS * CHUNKS)],
-            *[pltpu.VMEM((CHUNKS, EARLY, rows, blk), bf16) for _ in range(2 * STEPS)],
+            *[pltpu.VMEM((8, rows, blk), bf16) for _ in range(STEPS * CHUNKS)],
+            *[pltpu.VMEM((OWN, rows, blk), bf16) for _ in range(2 * STEPS * CHUNKS)],
+            *[
+                pltpu.VMEM((CHUNKS, count, rows, blk), bf16)
+                for count in (size - LATE, LATE, size - LATE, LATE)
+                for _ in range(STEPS)
+            ],
             *[pltpu.VMEM((own, blk, blk), f32) for _ in range(STEPS + 1)],
             pltpu.VMEM((own, blk, blk), f32),
             *[pltpu.VMEM(env, bf16) for _ in range(4)],
@@ -422,7 +495,7 @@
             pltpu.VMEM((len(ENTRIES), 8, blk), f32),
             pltpu.VMEM((3, 16, 128), f32),
             pltpu.VMEM((16, 128), f32),
-            pltpu.SMEM((HOPS * OWN + 2 * EARLY,), jnp.int32),
+            pltpu.SMEM((32,), jnp.int32),
             dma((5,)),
             dma((STEPS, CHUNKS, 4)),
             dma((STEPS, CHUNKS, 3)),
@@ -432,9 +505,9 @@
             dma((2, 2, own)),
         ],
         compiler_params=pltpu.CompilerParams(
-            collective_id=0, has_side_effects=True, vmem_limit_bytes=61_700_000
+            collective_id=index, has_side_effects=True, vmem_limit_bytes=61_700_000
         ),
-    )(kept_rank, step_size, hop_source, *held)
+    )(kept_rank, step_size, hop_source, plan, *held)
     return pl.pallas_call(
         write_out,
         out_shape=tuple(jax.ShapeDtypeStruct(shape, f32) for shape in shapes),
@@ -443,6 +516,17 @@
         scratch_shapes=[dma((3, own))],
         compiler_params=pltpu.CompilerParams(vmem_limit_bytes=8 * 1024 * 1024),
     )(*[pltpu.with_memory_space_constraint(x, pltpu.VMEM) for x in results])
+
+
+def on_device(*args):
+    smem = pl.BlockSpec(memory_space=pltpu.SMEM)
+    plan, choice = pl.pallas_call(
+        plan_kernel,
+        out_shape=(jax.ShapeDtypeStruct((4,), jnp.int32), jax.ShapeDtypeStruct((1,), jnp.int32)),
+        in_specs=[smem],
+        out_specs=(smem, smem),
+    )(args[-1])
+    return lax.switch(choice.reshape(()), [functools.partial(window, i) for i in range(len(SIZES))], plan, *args)
 
 
 def solution(mesh):

time: 141 us -> 139 us (0.986)
  the two profiles are of different devices: /device:TPU:40 before, /device:TPU:245 now
where the time goes in v4:
time: 139 us; the launch traced here: 140 us
  Pallas kernels  138 us (99%)
  between operations  1.47 us (1%)
    pallas_call x1, Pallas kernels, window(): pl.pallas_call(functools.partial(kernel, size), out_shape=tuple((pltpu.VM...  134 us

profile of v4, /device:TPU:245, one launch (start us, length us, event | category | flops | bytes accessed | tf_op | source)
XLA Modules:
  0.0 140.1 jit_solution(13371485115327311794)
XLA Ops:
  0.6 1.3 shard_map.112
  2.6 137.3 %conditional.1 = ((f32[1,4,256,256]{3,2,1,0:T(8,128)}, f32[1,2,4,256,256]{4,3,2,1,0:T(8,128)}, f32[1,2,4,256,256]{4,3,2,1,0:T(8,128)})) conditional(s32[]{:T(128)} %bitcast, (s32[1,4]{1,0:T(1,128)}, f32[1,3]{1,0:T(1,128)}, s32[2,16]{1,0:T(2,128)}, s32[4]{0:T(128)S(1)}, f32[1,4,256,256]{3,2,1,0:T(8,128)}, ...), branch_computations={%region_0.0_spmd, %region_1.0_spmd, %region_2.0_spmd} | conditional | bytes 8 | solution.py:529
  2.9 134.3 %branch_2_fun.2 = (f32[1,4,256,256]{3,2,1,0:T(8,128)S(1)}, f32[1,2,4,256,256]{4,3,2,1,0:T(8,128)S(1)}, f32[1,2,4,256,256]{4,3,2,1,0:T(8,128)S(1)}) custom-call(s32[1,4]{1,0:T(1,128)} %get-tuple-element.78.rank, f32[1,3]{1,0:T(1,128)} %get-tuple-element.79.step_size, s32[2,16]{1,0:T(2,128)} %get-tuple-element.80.source, s32[4]{0:T(128)S(1)} %get-tuple-element.81.plan, ...), custom_call_target="tpu_custom_call" | custom-call | tf_op jit(solution)/shard_map/cond/branch_2_fun/pallas_call | solution.py:478
  137.2 2.5 %branch_2_fun.3 = (f32[1,4,256,256]{3,2,1,0:T(8,128)}, f32[1,2,4,256,256]{4,3,2,1,0:T(8,128)}, f32[1,2,4,256,256]{4,3,2,1,0:T(8,128)}) custom-call(f32[1,4,256,256]{3,2,1,0:T(8,128)S(1)} %get-tuple-element.87.refs_0_, f32[1,2,4,256,256]{4,3,2,1,0:T(8,128)S(1)} %get-tuple-element.88.refs_1_, f32[1,2,4,256,256]{4,3,2,1,0:T(8,128)S(1)} %get-tuple-element.89.refs_2_), custom_call_target="tpu_custom_call" | custom-call | tf_op jit(solution)/shard_map/cond/branch_2_fun/pallas_call | solution.py:511

commit v5 on v4

--- a/solution.py
+++ b/solution.py
@@ -15,7 +15,7 @@
 SIZES = (8, 7, 6)
 CHUNKS = 8
 RELAY_LAG = CHUNKS - 2
-LATE_LAG = 2
+LATE_LAG = 3
 ENTRIES = tuple((i, j) for j in range(STEPS + 1) for i in range(j + 1))
 
 
@@ -363,11 +363,11 @@
         scale = 1.0 / jnp.sqrt(quadratic(new, new, gram, 0, 0))
         coef = [c * scale for c in new]
 
-    def merge(direction, a, j):
+    def merge(direction, j):
         src, dst, to = ((send_left, from_left, nxt), (send_right, from_right, prv))[direction]
         return pltpu.make_async_remote_copy(
-            src_ref=src.at[a, j], dst_ref=dst.at[a, j], send_sem=merge_send.at[direction, a, j],
-            recv_sem=merge_recv.at[direction, a, j], device_id=(to, z), device_id_type=MESH,
+            src_ref=src.at[j], dst_ref=dst.at[j], send_sem=merge_send.at[direction, j],
+            recv_sem=merge_recv.at[direction, j], device_id=(to, z), device_id_type=MESH,
         )
 
     def finish(j, carry):
@@ -379,38 +379,35 @@
         own_t = value.T.astype(bf16)
         for a in range(2):
             half = dot(own_t, left[a, j]).astype(bf16)
-            send_left[a, j] = (chi * dot(half, own)).astype(bf16)
+            send_left[j, a] = (chi * dot(half, own)).astype(bf16)
             half = dot(right[a, j], own_t).astype(bf16)
-            send_right[a, j] = (chi * dot(own, half)).astype(bf16)
+            send_right[j, a] = (chi * dot(own, half)).astype(bf16)
 
         @pl.when(has_next)
         def _():
-            for a in range(2):
-                merge(0, a, j).start()
+            merge(0, j).start()
 
         @pl.when(has_prev)
         def _():
-            for a in range(2):
-                merge(1, a, j).start()
+            merge(1, j).start()
 
         return carry
 
     lax.fori_loop(0, OWN, finish, 0, unroll=True)
-    def receive(direction, a, j, out, env, got):
-        merge(direction, a, j).wait_recv()
-        out[0, a, j] = env[a, j].astype(f32) + got[a, j].astype(f32)
+    def receive(direction, j, out, env, got):
+        merge(direction, j).wait_recv()
+        for a in range(2):
+            out[0, a, j] = env[a, j].astype(f32) + got[j, a].astype(f32)
 
     @pl.when(has_prev)
     def _():
         for j in range(OWN):
-            for a in range(2):
-                receive(0, a, j, merged_left, left, from_left)
+            receive(0, j, merged_left, left, from_left)
 
     @pl.when(has_next)
     def _():
         for j in range(OWN):
-            for a in range(2):
-                receive(1, a, j, merged_right, right, from_right)
+            receive(1, j, merged_right, right, from_right)
 
     @pl.when(jnp.logical_not(has_prev))
     def _():
@@ -440,15 +437,13 @@
 
     @pl.when(has_next)
     def _():
-        for a in range(2):
-            for j in range(OWN):
-                merge(0, a, j).wait_send()
+        for j in range(OWN):
+            merge(0, j).wait_send()
 
     @pl.when(has_prev)
     def _():
-        for a in range(2):
-            for j in range(OWN):
-                merge(1, a, j).wait_send()
+        for j in range(OWN):
+            merge(1, j).wait_send()
 
 
 def write_out(*refs):
@@ -491,7 +486,7 @@
             *[pltpu.VMEM((own, blk, blk), f32) for _ in range(STEPS + 1)],
             pltpu.VMEM((own, blk, blk), f32),
             *[pltpu.VMEM(env, bf16) for _ in range(4)],
-            *[pltpu.VMEM(env, bf16) for _ in range(4)],
+            *[pltpu.VMEM((own, 2, blk, blk), bf16) for _ in range(4)],
             pltpu.VMEM((len(ENTRIES), 8, blk), f32),
             pltpu.VMEM((3, 16, 128), f32),
             pltpu.VMEM((16, 128), f32),
@@ -501,8 +496,8 @@
             dma((STEPS, CHUNKS, 3)),
             dma((3,)),
             dma((3,)),
-            dma((2, 2, own)),
-            dma((2, 2, own)),
+            dma((2, own)),
+            dma((2, own)),
         ],
         compiler_params=pltpu.CompilerParams(
             collective_id=index, has_side_effects=True, vmem_limit_bytes=61_700_000

time: 139 us -> 133 us (0.957)
  the two profiles are of different devices: /device:TPU:245 before, /device:TPU:40 now
where the time goes in v5:
time: 133 us; the launch traced here: 132 us
  Pallas kernels  130 us (98%)
  between operations  1.47 us (1%)
    pallas_call x1, Pallas kernels, window(): pl.pallas_call(functools.partial(kernel, size), out_shape=tuple((pltpu.VM...  127 us

profile of v5, /device:TPU:40, one launch (start us, length us, event | category | flops | bytes accessed | tf_op | source)
XLA Modules:
  0.0 132.3 jit_solution(3492487046058649219)
XLA Ops:
  0.6 1.3 shard_map.112
  2.6 129.6 %conditional.1 = ((f32[1,4,256,256]{3,2,1,0:T(8,128)}, f32[1,2,4,256,256]{4,3,2,1,0:T(8,128)}, f32[1,2,4,256,256]{4,3,2,1,0:T(8,128)})) conditional(s32[]{:T(128)} %bitcast, (s32[1,4]{1,0:T(1,128)}, f32[1,3]{1,0:T(1,128)}, s32[2,16]{1,0:T(2,128)}, s32[4]{0:T(128)S(1)}, f32[1,4,256,256]{3,2,1,0:T(8,128)}, ...), branch_computations={%region_0.0_spmd, %region_1.0_spmd, %region_2.0_spmd} | conditional | bytes 8 | solution.py:524
  2.6 126.6 %branch_1_fun.2 = (f32[1,4,256,256]{3,2,1,0:T(8,128)S(1)}, f32[1,2,4,256,256]{4,3,2,1,0:T(8,128)S(1)}, f32[1,2,4,256,256]{4,3,2,1,0:T(8,128)S(1)}) custom-call(s32[1,4]{1,0:T(1,128)} %get-tuple-element.66.rank, f32[1,3]{1,0:T(1,128)} %get-tuple-element.67.step_size, s32[2,16]{1,0:T(2,128)} %get-tuple-element.68.source, s32[4]{0:T(128)S(1)} %get-tuple-element.69.plan, ...), custom_call_target="tpu_custom_call" | custom-call | tf_op jit(solution)/shard_map/cond/branch_1_fun/pallas_call | solution.py:473
  129.2 2.5 %branch_1_fun.3 = (f32[1,4,256,256]{3,2,1,0:T(8,128)}, f32[1,2,4,256,256]{4,3,2,1,0:T(8,128)}, f32[1,2,4,256,256]{4,3,2,1,0:T(8,128)}) custom-call(f32[1,4,256,256]{3,2,1,0:T(8,128)S(1)} %get-tuple-element.75.refs_0_, f32[1,2,4,256,256]{4,3,2,1,0:T(8,128)S(1)} %get-tuple-element.76.refs_1_, f32[1,2,4,256,256]{4,3,2,1,0:T(8,128)S(1)} %get-tuple-element.77.refs_2_), custom_call_target="tpu_custom_call" | custom-call | tf_op jit(solution)/shard_map/cond/branch_1_fun/pallas_call | solution.py:506
